TPU v7x, 512 devices: a whole 4x4x16 slice. The times are simulated.
512 devices in a mesh: pw: 32 (over y_lo, z), band: 16 (over y_hi, x, core).
Axes of the slice: x: 4, y: 4 (y_hi: 2, y_lo: 2; y = y_hi * 2 + y_lo), z: 16, core: 2. Of those that a mesh axis runs over, the one named last changes fastest.
Arguments:
- psi_occ: bfloat16 [2, 256, 49152], P(None, 'band', 'pw'), may hold values from -0.2890625 to 0.2890625
- psi_high: bfloat16 [2, 4096, 49152], P(None, 'band', 'pw'), may hold values from -0.2890625 to 0.2890625
- miller: int32 [3, 49152], P(None, 'pw'), may hold values from -24 to 24
- recip: float32 [3, 3], replicated, may hold values from -0.1 to 0.1
- kfrac: float32 [3], replicated, may hold values from -0.5 to 0.5
- positions: float32 [48, 3], replicated, may hold values from 0 to 20
- atom_type: int32 [48], replicated, may hold values from 0 to 2
- proj_atom: int32 [192], replicated, may hold values from 0 to 47
- widths: float32 [3], replicated, may hold values from 0.2 to 2
- dion: float32 [3], replicated, may hold values from 0.03 to 0.15
Outputs:
- dipole: float32 [3, 2, 256, 4096], P(None, None, 'pw', 'band')
All inputs are finite; a program needn't handle non-finite values.
Results may differ from a plain program's by a relative error of at most 0.0046.
Values may be sent and summed in bfloat16 or wider, within the bound.
A program may use at most 64 MiB of HBM per device.

v0:
```python
import jax
import jax.numpy as jnp
from jax import lax
from jax.sharding import PartitionSpec as P


def wave_vectors(miller, recip, kfrac):
    shifted = miller.astype(jnp.float32) + kfrac[:, None]
    return (
        shifted[0][None, :] * recip[0][:, None]
        + shifted[1][None, :] * recip[1][:, None]
        + shifted[2][None, :] * recip[2][:, None]
    )


def build_projectors(wavevec, centers, spread, channel):
    square = jnp.sum(wavevec * wavevec, axis=0)
    envelope = jnp.exp(-0.5 * spread[:, None] * square[None, :])
    selectors = [(channel == channel_id).astype(jnp.float32)[:, None] for channel_id in range(4)]
    angular = (
        selectors[0]
        + selectors[1] * wavevec[0][None, :]
        + selectors[2] * wavevec[1][None, :]
        + selectors[3] * wavevec[2][None, :]
    )
    phases = (
        centers[:, 0:1] * wavevec[0][None, :]
        + centers[:, 1:2] * wavevec[1][None, :]
        + centers[:, 2:3] * wavevec[2][None, :]
    )
    cosine_part = jnp.cos(phases)
    sine_part = jnp.sin(phases)
    radial = envelope * angular
    stacked_kinds = [jnp.concatenate([radial * cosine_part, -radial * sine_part], axis=1)]
    for direction in range(3):
        factor = envelope * (
            selectors[direction + 1] - spread[:, None] * wavevec[direction][None, :] * angular
        )
        stacked_kinds.append(jnp.concatenate([factor * sine_part, factor * cosine_part], axis=1))
    return jnp.stack(stacked_kinds).astype(jnp.bfloat16)


def pair_forms(values):
    return jnp.stack(
        [
            jnp.concatenate([values[0], values[1]], axis=-1),
            jnp.concatenate([values[1], -values[0]], axis=-1),
        ]
    )


def swapped(values):
    return jnp.stack([values[:, 1], -values[:, 0]], axis=1)


def nonlocal_terms(occ_weighted, high_coef):
    hp = lax.Precision.HIGHEST
    real_part = jnp.einsum(
        "cmi,acin->amn", occ_weighted[0], high_coef[1:], precision=hp
    ) - jnp.einsum("acmi,cin->amn", occ_weighted[1:], high_coef[0], precision=hp)
    other = swapped(high_coef)
    imag_part = jnp.einsum("cmi,acin->amn", occ_weighted[0], other[1:], precision=hp) - jnp.einsum(
        "acmi,cin->amn", occ_weighted[1:], other[0], precision=hp
    )
    return (real_part, imag_part)


def on_device(
    psi_occ, psi_high, miller, recip, kfrac, positions, atom_type, proj_atom, widths, dion
):
    hp = lax.Precision.HIGHEST
    band_count = lax.axis_size("band")
    band_id = lax.axis_index("band")
    proj_total = proj_atom.shape[0]
    own_proj = proj_total // band_count
    width_local = psi_occ.shape[2]
    atom_hot = (
        proj_atom[:, None] == jnp.arange(positions.shape[0], dtype=jnp.int32)[None, :]
    ).astype(jnp.float32)
    type_hot = (atom_type[:, None] == jnp.arange(widths.shape[0], dtype=jnp.int32)[None, :]).astype(
        jnp.float32
    )
    centers = jnp.dot(atom_hot, positions, precision=hp)
    proj_type = jnp.dot(atom_hot, type_hot, precision=hp)
    spread = jnp.dot(proj_type, widths, precision=hp)
    strength = jnp.dot(proj_type, dion, precision=hp)
    channel = jnp.arange(proj_total, dtype=jnp.int32) % 4
    wavevec = wave_vectors(miller, recip, kfrac)
    high_pair = pair_forms(psi_high)
    own_start = band_id * own_proj
    own_projectors = build_projectors(
        wavevec,
        lax.dynamic_slice_in_dim(centers, own_start, own_proj, 0),
        lax.dynamic_slice_in_dim(spread, own_start, own_proj, 0),
        lax.dynamic_slice_in_dim(channel, own_start, own_proj, 0),
    )
    proj_pair = jnp.stack(
        [
            own_projectors,
            jnp.concatenate(
                [-own_projectors[:, :, width_local:], own_projectors[:, :, :width_local]], axis=-1
            ),
        ],
        axis=1,
    )
    block_size = proj_total // 4
    coef_blocks = []
    for block_id in range(4):
        lower = block_id * block_size
        block_projectors = build_projectors(
            wavevec,
            centers[lower : lower + block_size],
            spread[lower : lower + block_size],
            channel[lower : lower + block_size],
        )
        coef_blocks.append(
            jnp.einsum(
                "kig,cng->kcin", block_projectors, high_pair, preferred_element_type=jnp.float32
            )
        )
    high_partial = jnp.concatenate(coef_blocks, axis=2)
    occ_piece = lax.all_gather(psi_occ, "band", axis=1, tiled=True)
    occ_cat = jnp.concatenate([occ_piece[0], occ_piece[1]], axis=-1)
    parts = []
    for direction in range(3):
        doubled = jnp.concatenate([wavevec[direction], wavevec[direction]])
        scaled = (doubled[None, :] * occ_cat.astype(jnp.float32)).astype(jnp.bfloat16)
        parts.append(
            jnp.einsum("rg,cng->crn", scaled, high_pair, preferred_element_type=jnp.float32)
        )
    momentum = jnp.stack(parts)
    coef_part = jnp.einsum("kcig,rg->kcri", proj_pair, occ_cat, preferred_element_type=jnp.float32)
    occ_coef = coef_part
    momentum, occ_coef = (momentum, occ_coef)
    high_coef = lax.psum(high_partial, "pw")
    momentum, occ_coef = (
        lax.psum_scatter(momentum, "pw", scatter_dimension=2, tiled=True),
        lax.psum_scatter(occ_coef, "pw", scatter_dimension=2, tiled=True),
    )
    occ_all = lax.all_gather(occ_coef, "band", axis=3, tiled=True)
    occ_weighted = occ_all * strength[None, None, None, :]
    real_part, imag_part = nonlocal_terms(occ_weighted, high_coef)
    return jnp.stack([momentum[:, 0] - imag_part, momentum[:, 1] + real_part], axis=1)


def solution(mesh):
    placed = (
        P(None, "band", "pw"),
        P(None, "band", "pw"),
        P(None, "pw"),
        P(),
        P(),
        P(),
        P(),
        P(),
        P(),
        P(),
    )
    return jax.shard_map(
        on_device,
        mesh=mesh,
        in_specs=placed,
        out_specs=P(None, None, "pw", "band"),
        check_vma=False,
    )
```

profile of v0, /device:TPU:1, one launch (start us, length us, event | category | flops | bytes accessed | tf_op | source)
XLA Modules:
  0.0 406.0 jit_solution(5235723133159526868)
XLA Ops:
  6.5 0.7 all-gather.2.cloned.1.call-update
  7.3 1.6 slice_bitcast_fusion.3
  12.3 1.6 multiply_convert_fusion.31
  14.1 1.6 multiply_convert_fusion.23
  15.8 1.2 fusion.38
  17.0 1.2 fusion.41
  18.2 1.6 multiply_convert_fusion.15
  19.9 1.2 fusion.44
  21.1 1.6 multiply_convert_fusion.7
  22.9 1.2 fusion.47
  24.1 1.3 pad_maximum_fusion.3
  26.0 0.7 fusion.128
  26.7 0.7 fusion.124
  27.6 51.0 %all-gather.2.cloned.1.call-done = bf16[2,256,1536]{2,1,0:T(8,128)(2,1)} async-done(((bf16[2,16,1536]{2,1,0:T(8,128)(2,1)}), bf16[2,256,1536]{2,1,0:T(8,128)(2,1)}) %all-gather.2.cloned.1.call-update) | async-done | bytes 1572880 | tf_op jit(solution)/shard_map/all_gather | solution.py:122
  78.6 1.5 slice_bitcast_fusion.1
  80.1 0.9 copy-done.7
  81.4 1.3 fusion.74
  82.7 2.2 copy.35
  84.9 2.6 fusion.29
  87.5 1.0 fusion.32
  88.6 1.0 fusion.35
  89.8 2.2 copy.33
  92.0 1.3 dynamic-slice
  94.1 249.7 %all-reduce.5.cloned.1.call-done = (f32[4,2,256,12]{3,0,1,2:T(4,128)}, f32[4,2,192,256]{3,2,0,1:T(8,128)}, f32[3,2,256,256]{3,1,0,2:T(2,128)}) async-done(((f32[4,2,256,12]{3,0,1,2:T(4,128)}, f32[4,2,192,256]{3,2,0,1:T(8,128)}, f32[3,2,256,256]{3,1,0,2:T(2,128)}), (f32[4,2,256,12]{3,0,1,2:T(4,128)}, f32[4,2,192,256]{3,2,0,1:T(8,128)}, f32[3,2,256,256]{3,1,0,2:T(2,128)})) %all-reduce.5.cloned.1.call-update) | async-done | bytes 3244048
  343.8 1.5 fusion.144
  345.4 0.9 constant_dynamic-slice_fusion.1
  346.4 47.6 %all_gather.7 = f32[4,2,8,192]{2,0,1,3:T(4,128)} all-gather(f32[4,2,8,12]{2,0,1,3:T(4,128)S(1)} %copy.36), channel_id=1, replica_groups=mesh['pw'=32,'band'=16] {'band'}, dimensions={3}, use_global_device_ids=true | all-gather | bytes 52224 | tf_op jit(solution)/shard_map/all_gather | solution.py:140
  394.0 1.4 copy.37
  395.8 0.7 fusion.80
  396.5 0.9 constant_dynamic-slice_fusion
  397.8 0.7 fusion.79
  398.5 0.6 pad_maximum_fusion.5
  (91 shorter events, 6.0 us)
Async XLA Ops:
  6.5 2.8 copy-start
  6.5 72.0 %all-gather.2.cloned.1.call-start = ((), (), s32[]{:S(2)}) async-start(), calls=%async_computation | async-start | bytes 1671168 | tf_op jit(solution)/shard_map/all_gather | solution.py:122
  7.3 336.6 %all-reduce.5.cloned.1.call-start = ((), (), s32[]{:S(2)}) async-start(), calls=%async_computation.1 | async-start | bytes 8388608
  7.3 1.9 copy-start.2
  9.2 0.7 copy-start.19
  9.2 1.2 copy-start.15
  9.2 1.2 copy-start.18
  9.2 1.3 copy-start.17
  9.2 1.5 copy-start.20
  9.2 1.8 copy-start.21
  11.0 1.3 copy-start.23
  12.3 10.6 %copy-start.3 = (bf16[1,256,3072]{2,1,0:T(8,128)(2,1)}, bf16[1,256,3072]{2,1,0:T(8,128)(2,1)S(1)}, u32[]{:S(2)}) copy-start(bf16[1,256,3072]{2,1,0:T(8,128)(2,1)S(1)} %get-tuple-element.28) | copy-start | bytes 4718596
  12.3 10.6 %copy-start.5 = (bf16[1,256,3072]{2,1,0:T(8,128)(2,1)}, bf16[1,256,3072]{2,1,0:T(8,128)(2,1)S(1)}, u32[]{:S(2)}) copy-start(bf16[1,256,3072]{2,1,0:T(8,128)(2,1)S(1)} %get-tuple-element.29) | copy-start | bytes 4718596
  78.6 2.7 copy-start.11
  78.6 2.7 copy-start.12
  78.6 2.7 copy-start.13
  78.6 2.7 copy-start.14
  80.1 0.9 copy-start.7
  80.1 1.2 copy-start.9
  81.3 3.6 copy-start.4
  81.3 3.6 copy-start.6
  84.9 2.6 copy-start.8
  84.9 2.6 copy-start.10
  84.9 2.6 copy-start.16
  92.0 2.0 copy-start.22
  92.0 2.0 copy-start.24
  345.4 50.1 %copy-start.1 = (f32[4,2,192,256]{3,2,0,1:T(8,128)S(1)}, f32[4,2,192,256]{3,2,0,1:T(8,128)}, u32[]{:S(2)}) copy-start(f32[4,2,192,256]{3,2,0,1:T(8,128)} %get-tuple-element.12) | copy-start | bytes 4718596
Sparse Core Ops, SparseCore 0:
  10.7 67.8 all-gather.1
  92.2 251.6 all-reduce.4
where the time goes:
time: 406 us
  waiting for transfers between devices  301 us (74%)
  blocking collectives  47.6 us (12%)
  local copies, waits for them, and re-layouts  14.6 us (4%)
  between operations  14.5 us (4%)
  other arithmetic  14.3 us (4%)
  matrix products  13.5 us (3%)
    unnamed x3, waiting for transfers between devices  250 us
    all_gather x1, waiting for transfers between devices, on_device(): occ_piece = lax.all_gather(psi_occ, 'band', axis=1, tiled=True)  51 us
    all_gather x1, blocking collectives, on_device(): occ_all = lax.all_gather(occ_coef, 'band', axis=3, tiled=True)  47.6 us
  transfers between devices with their start and end apart: 2, of which 2 were waited for; matrix products, arithmetic and copies ran while one was open for 5% of the time, Pallas kernels for 0%

commit v1 on v0

v1 whole, which is shorter than its diff:
```python
import functools

import jax
import jax.numpy as jnp
from jax import lax
from jax.experimental import pallas as pl
from jax.experimental.pallas import tpu as pltpu
from jax.sharding import PartitionSpec as P

MESH = pl.DeviceIdType.MESH
F32 = jnp.float32
BF16 = jnp.bfloat16
LANES = 512


def projector_table(positions, atom_type, proj_atom, widths, dion):
    hp = lax.Precision.HIGHEST
    atom_hot = (
        proj_atom[:, None] == jnp.arange(positions.shape[0], dtype=jnp.int32)[None, :]
    ).astype(F32)
    type_hot = (atom_type[:, None] == jnp.arange(widths.shape[0], dtype=jnp.int32)[None, :]).astype(F32)
    per_type = jnp.stack([widths, dion], axis=1)
    per_atom = jnp.concatenate([positions, jnp.dot(type_hot, per_type, precision=hp)], axis=1)
    return jnp.dot(atom_hot, per_atom, precision=hp)


def sin_cos(angle):
    turns = jnp.floor(angle * 0.6366197723675814 + 0.5)
    rest = angle - turns * 1.5703125
    rest = rest - turns * 4.837512969970703125e-4
    rest = rest - turns * 7.54978995489188216e-8
    square = rest * rest
    sine = rest + rest * square * (
        -1.6666654611e-1 + square * (8.3321608736e-3 + square * -1.9515295891e-4)
    )
    cosine = (
        1.0
        - 0.5 * square
        + square * square * (4.166664568298827e-2 + square * (-1.388731625493765e-3 + square * 2.443315711809948e-5))
    )
    quadrant = turns - 4.0 * jnp.floor(turns * 0.25)
    odd = (quadrant == 1.0) | (quadrant == 3.0)
    first = jnp.where(odd, cosine, sine)
    second = jnp.where(odd, sine, cosine)
    sine = jnp.where(quadrant >= 2.0, -first, first)
    cosine = jnp.where((quadrant == 1.0) | (quadrant == 2.0), -second, second)
    return sine, cosine


def dot_t(lhs, rhs):
    return lax.dot_general(lhs, rhs, (((1,), (1,)), ((), ())), preferred_element_type=F32)


def kernel(
    nz,
    nx,
    occ_ref,
    high_ref,
    miller_ref,
    par_ref,
    strength_ref,
    recip_ref,
    kfrac_ref,
    out_ref,
    occ_all,
    wave,
    stage,
    proj,
    occ_a,
    occ_b,
    coef,
    occ_coef,
    occ_tile,
    scaled,
    total,
    ys1,
    yr1,
    oyr,
    us1,
    ur1,
    ds1,
    dr1,
    ys2,
    yr2,
    us2,
    ur2,
    ds2,
    dr2,
    tile_own,
    tiles,
    g_send,
    g_recv,
    y1_send,
    y1_recv,
    oy_send,
    oy_recv,
    u1_send,
    u1_recv,
    d1_send,
    d1_recv,
    y2_send,
    y2_recv,
    u2_send,
    u2_recv,
    d2_send,
    d2_recv,
    t_send,
    t_recv,
):
    p = lax.axis_index("pw")
    b = lax.axis_index("band")
    nband = 4 * nx
    y_lo, z = p // nz, p % nz
    y_hi, x, core = b // (2 * nx), (b // 2) % nx, b % 2
    half = nz // 2
    width = high_ref.shape[2]

    def band_id(yy, xx, cc):
        return yy * (2 * nx) + xx * 2 + cc

    def pw_id(yy, zz):
        return yy * nz + zz

    def put(src, dst, send, recv, pw, band):
        return pltpu.make_async_remote_copy(
            src_ref=src,
            dst_ref=dst,
            send_sem=send,
            recv_sem=recv,
            device_id={"pw": pw, "band": band},
            device_id_type=MESH,
        )

    y_mate = pw_id(1 - y_lo, z)
    z_up = pw_id(y_lo, (z + 1) % nz)
    z_down = pw_id(y_lo, (z + nz - 1) % nz)

    barrier = pltpu.get_barrier_semaphore()
    for pw in (y_mate, z_up, z_down):
        pl.semaphore_signal(barrier, inc=1, device_id={"pw": pw, "band": b}, device_id_type=MESH)
    for step in range(1, nband):
        pl.semaphore_signal(
            barrier, inc=1, device_id={"pw": p, "band": (b + step) % nband}, device_id_type=MESH
        )
    pl.semaphore_wait(barrier, 3 + nband - 1)

    started = []

    def forward(src, block, count, bands):
        for band in bands:
            copy = put(src, occ_all.at[block], g_send.at[count], g_recv.at[block], p, band)
            copy.start()
            started.append(copy)
            count += 1
        return count

    def block_arrived(block):
        put(occ_all.at[block], occ_all.at[block], g_send.at[0], g_recv.at[block], p, b).wait_recv()

    mate_block = band_id(1 - y_hi, x, core)
    x_others = [(x + dx) % nx for dx in range(1, nx)]
    sent = forward(
        occ_ref,
        b,
        0,
        [mate_block] + [band_id(y_hi, xx, core) for xx in x_others] + [band_id(y_hi, x, 1 - core)],
    )
    occ_all[b] = occ_ref[...]

    shifted = [miller_ref[axis : axis + 1, :].astype(F32) + kfrac_ref[axis] for axis in range(3)]
    vectors = [
        shifted[0] * recip_ref[0, axis] + shifted[1] * recip_ref[1, axis] + shifted[2] * recip_ref[2, axis]
        for axis in range(3)
    ]
    for axis in range(3):
        wave[axis] = jnp.broadcast_to(vectors[axis], (8, width))
    wave[3] = jnp.broadcast_to(
        vectors[0] * vectors[0] + vectors[1] * vectors[1] + vectors[2] * vectors[2], (8, width)
    )
    nown = occ_ref.shape[1]
    occ_a[...] = jnp.zeros_like(occ_a)
    occ_b[...] = jnp.zeros_like(occ_b)
    occ_a[0:nown, :] = occ_ref[0]
    occ_a[nown : 2 * nown, :] = occ_ref[1]
    occ_b[0:nown, :] = occ_ref[1]
    occ_b[nown : 2 * nown, :] = -occ_ref[0]

    channel = lax.broadcasted_iota(jnp.int32, (8, LANES), 0) % 4
    selectors = [(channel == value).astype(F32) for value in range(4)]
    pieces = width // LANES

    def place(part, kind, value):
        for piece in range(LANES // 128):
            stage[part, piece, pl.ds(kind, 8, stride=4), :] = value[:, 128 * piece : 128 * piece + 128]

    def build(index, carry):
        block = index // pieces
        columns = pl.ds(pl.multiple_of((index % pieces) * LANES, LANES), LANES)
        table = par_ref[pl.ds(pl.multiple_of(block * 8, 8), 8), :]
        k = [wave[axis, :, columns] for axis in range(3)]
        square = wave[3, :, columns]
        spread = table[:, 3:4]
        envelope = jnp.exp(-0.5 * spread * square)
        angular = selectors[0] + selectors[1] * k[0] + selectors[2] * k[1] + selectors[3] * k[2]
        sine, cosine = sin_cos(table[:, 0:1] * k[0] + table[:, 1:2] * k[1] + table[:, 2:3] * k[2])
        radial = envelope * angular
        place(0, 0, radial * cosine)
        place(1, 0, -radial * sine)
        for axis in range(3):
            factor = envelope * (selectors[axis + 1] - spread * k[axis] * angular)
            place(0, axis + 1, factor * sine)
            place(1, axis + 1, factor * cosine)
        rows = pl.ds(pl.multiple_of(block * 32, 32), 32)
        for part in range(2):
            pieces_of = [stage[part, piece] for piece in range(LANES // 128)]
            proj[part, rows, columns] = jnp.concatenate(pieces_of, axis=1).astype(BF16)
        return carry

    lax.fori_loop(0, (par_ref.shape[0] // 8) * pieces, build, 0)

    block_arrived(mate_block)
    sent = forward(
        occ_all.at[mate_block],
        mate_block,
        sent,
        [band_id(y_hi, xx, core) for xx in x_others] + [band_id(y_hi, x, 1 - core)],
    )

    coef[...] = jnp.zeros_like(coef)
    occ_coef[...] = jnp.zeros_like(occ_coef)

    def project(index, carry):
        columns = pl.ds(pl.multiple_of(index * 256, 256), 256)
        real, imag = proj[0, :, columns], proj[1, :, columns]
        high_r, high_i = high_ref[0, :, columns], high_ref[1, :, columns]
        occ_coef[...] += dot_t(real, occ_a[:, columns]) + dot_t(imag, occ_b[:, columns])
        coef[0] += dot_t(real, high_r) + dot_t(imag, high_i)
        coef[1] += dot_t(real, high_i) - dot_t(imag, high_r)
        return carry

    lax.fori_loop(0, width // 256, project, 0)

    npw = 2 * nz
    for owner in range(npw):
        rows = occ_coef[24 * owner : 24 * owner + 24, :] * strength_ref[24 * owner : 24 * owner + 24, :]
        occ_tile[owner] = (
            rows[0:8] + pltpu.roll(rows[8:16], 32, 1) + pltpu.roll(rows[16:24], 64, 1)
        )

    def chunk1(owner):
        return coef[:, pl.ds(pl.multiple_of(owner * 24, 8), 24), :].reshape(48, 256)

    def chunk2(owner):
        return total[:, :, pl.ds(pl.multiple_of(owner * 8, 8), 8), :].reshape(48, 256)

    def up_dest(step):
        return (z + half - step + nz) % nz

    def down_dest(step):
        return (z + half + 1 + step) % nz

    def mate_sends(chunk, ys, yr, send, recv):
        copies = []
        for step in range(half):
            ys[step, 0] = chunk(pw_id(1 - y_lo, up_dest(step))).astype(BF16)
            ys[step, 1] = chunk(pw_id(1 - y_lo, down_dest(step))).astype(BF16)
            copy = put(ys.at[step], yr.at[step], send.at[step], recv.at[step], y_mate, b)
            copy.start()
            copies.append(copy)
        return copies

    tile_copy = put(
        occ_tile.at[pl.ds((1 - y_lo) * nz, nz)], oyr, oy_send.at[0], oy_recv.at[0], y_mate, b
    )
    tile_copy.start()
    mates1 = mate_sends(chunk1, ys1, yr1, y1_send, y1_recv)

    def occ_sum(dest):
        tile = occ_tile[pw_id(y_lo, dest)] + oyr[dest]
        return jnp.concatenate([tile, jnp.zeros_like(tile)], axis=1)

    for yy in (y_hi, 1 - y_hi):
        for xx in x_others:
            block = band_id(yy, xx, core)
            block_arrived(block)
            sent = forward(occ_all.at[block], block, sent, [band_id(y_hi, x, 1 - core)])
    tile_copy.wait_recv()
    total[...] = jnp.zeros_like(total)

    rings = []

    def ring_step(step, chunk, yr, mates, us, ur, ds, dr, u_send, u_recv, d_send, d_recv, tail):
        mates[step].wait_recv()
        if step > 0:
            rings_up[step - 1].wait_recv()
        dest = up_dest(step)
        value = chunk(pw_id(y_lo, dest)) + yr[step, 0].astype(F32)
        if step > 0:
            value = value + ur[step - 1, 0:48, :]
        us[step, 0:48, :] = value
        if tail:
            extra = occ_sum(dest)
            if step > 0:
                extra = extra + ur[step - 1, 48:56, :]
            us[step, 48:56, :] = extra
        copy = put(us.at[step], ur.at[step], u_send.at[step], u_recv.at[step], z_up, b)
        copy.start()
        rings_up.append(copy)
        if step < half - 1:
            if step > 0:
                rings_down[step - 1].wait_recv()
            dest = down_dest(step)
            value = chunk(pw_id(y_lo, dest)) + yr[step, 1].astype(F32)
            if step > 0:
                value = value + dr[step - 1, 0:48, :]
            ds[step, 0:48, :] = value
            if tail:
                extra = occ_sum(dest)
                if step > 0:
                    extra = extra + dr[step - 1, 48:56, :]
                ds[step, 48:56, :] = extra
            copy = put(ds.at[step], dr.at[step], d_send.at[step], d_recv.at[step], z_down, b)
            copy.start()
            rings_down.append(copy)

    def ring_end(chunk, yr, ur, dr):
        rings_up[half - 1].wait_recv()
        rings_down[half - 2].wait_recv()
        value = chunk(pw_id(y_lo, z)) + yr[half - 1, 1].astype(F32)
        return value + ur[half - 1, 0:48, :] + dr[half - 2, 0:48, :]

    nocc = total.shape[2]

    def momentum_piece(index):
        columns = pl.ds(pl.multiple_of(index * 256, 256), 256)
        for part in range(2):
            values = occ_all[:, part, :, columns].reshape(nocc, 256).astype(F32)
            for axis in range(3):
                vector = wave[axis, 0:1, columns]
                scaled[part, axis * nocc : (axis + 1) * nocc, :] = (values * vector).astype(BF16)
        real, imag = scaled[0], scaled[1]
        high_r, high_i = high_ref[0, :, columns], high_ref[1, :, columns]
        total[0] += (dot_t(real, high_r) + dot_t(imag, high_i)).reshape(3, nocc, 256)
        total[1] += (dot_t(real, high_i) - dot_t(imag, high_r)).reshape(3, nocc, 256)

    rings_up, rings_down = [], []
    ring_refs = (us1, ur1, ds1, dr1, u1_send, u1_recv, d1_send, d1_recv)
    ring_step(0, chunk1, yr1, mates1, *ring_refs, True)
    for xx in [x] + x_others:
        for yy in range(2):
            block_arrived(band_id(yy, xx, 1 - core))
    for step in range(1, half):
        ring_step(step, chunk1, yr1, mates1, *ring_refs, True)
        if step - 1 < width // 256:
            momentum_piece(step - 1)
    for index in range(half - 1, width // 256):
        momentum_piece(index)
    high_sum = ring_end(chunk1, yr1, ur1, dr1)
    tile_own[...] = (
        occ_tile[p] + oyr[z] + ur1[half - 1, 48:56, 0:128] + dr1[half - 2, 48:56, 0:128]
    )
    rings1 = rings_up + rings_down

    tile_copies = []
    for step in range(1, nband):
        copy = put(
            tile_own, tiles.at[b], t_send.at[step - 1], t_recv.at[b], p, (b + step) % nband
        )
        copy.start()
        tile_copies.append(copy)
    tiles[b] = tile_own[...]
    high_hi = high_sum.astype(BF16)
    high_lo = (high_sum - high_hi.astype(F32)).astype(BF16)
    rhs = jnp.concatenate([high_hi, high_lo, high_hi], axis=0)
    for step in range(1, nband):
        block = (b + step) % nband
        put(tile_own, tiles.at[block], t_send.at[0], t_recv.at[block], p, b).wait_recv()

    lane_block = lax.broadcasted_iota(jnp.int32, (8, 128), 1) // 16
    occ_sums = []
    for part in range(2):
        groups = []
        for group in range(3):
            halves = []
            for side in range(nband // 8):
                value = jnp.zeros((8, 128), F32)
                for place in range(8):
                    shift = (16 * place - 32 * group - 16 * part) % 128
                    tile = tiles[8 * side + place]
                    if shift:
                        tile = pltpu.roll(tile, shift, 1)
                    value = jnp.where(lane_block == place, tile, value)
                halves.append(value)
            groups.append(jnp.concatenate(halves, axis=1))
        occ_sums.append(jnp.concatenate(groups, axis=0))
    kind = lax.broadcasted_iota(jnp.int32, (24, 256), 0) % 4
    for axis in range(3):
        mixed = []
        for part in range(2):
            value = occ_sums[part]
            lower = pltpu.roll(value, axis + 1, 0)
            upper = pltpu.roll(value, 24 - (axis + 1), 0)
            mixed.append(
                jnp.where(kind == axis + 1, lower, jnp.where(kind == 0, -upper, jnp.zeros_like(value)))
            )
        for part in range(2):
            if part == 0:
                left = jnp.concatenate([mixed[1], -mixed[0]], axis=0)
            else:
                left = jnp.concatenate([mixed[0], mixed[1]], axis=0)
            left_hi = left.astype(BF16)
            left_lo = (left - left_hi.astype(F32)).astype(BF16)
            lhs = jnp.concatenate([left_hi, left_hi, left_lo], axis=0)
            total[part, axis] += lax.dot_general(
                lhs, rhs, (((0,), (0,)), ((), ())), preferred_element_type=F32
            )

    mates2 = mate_sends(chunk2, ys2, yr2, y2_send, y2_recv)
    rings_up, rings_down = [], []
    ring_refs = (us2, ur2, ds2, dr2, u2_send, u2_recv, d2_send, d2_recv)
    for step in range(half):
        ring_step(step, chunk2, yr2, mates2, *ring_refs, False)
    result = ring_end(chunk2, yr2, ur2, dr2).reshape(2, 3, 8, 256)
    for axis in range(3):
        for part in range(2):
            out_ref[axis, part] = result[part, axis]

    for copy in started + [tile_copy] + mates1 + rings1 + tile_copies + mates2 + rings_up + rings_down:
        copy.wait_send()


def on_device(
    nz, nx, psi_occ, psi_high, miller, recip, kfrac, positions, atom_type, proj_atom, widths, dion
):
    nproj = proj_atom.shape[0]
    nown, nhigh, width = psi_occ.shape[1], psi_high.shape[1], psi_high.shape[2]
    npw, nband, half = 2 * nz, 4 * nx, nz // 2
    nocc = nown * nband
    table = projector_table(positions, atom_type, proj_atom, widths, dion)
    strength = jnp.broadcast_to(jnp.repeat(table[:, 4:5], 4, axis=0), (4 * nproj, 128))
    vmem, smem = pltpu.VMEM, pltpu.SMEM
    dma = pltpu.SemaphoreType.DMA
    out = pl.pallas_call(
        functools.partial(kernel, nz, nx),
        out_shape=jax.ShapeDtypeStruct((3, 2, nocc // npw, nhigh), F32),
        in_specs=[pl.BlockSpec(memory_space=vmem)] * 5 + [pl.BlockSpec(memory_space=smem)] * 2,
        out_specs=pl.BlockSpec(memory_space=vmem),
        scratch_shapes=[
            vmem((nband, 2, nown, width), BF16),
            vmem((4, 8, width), F32),
            vmem((2, LANES // 128, 32, 128), F32),
            vmem((2, 4 * nproj, width), BF16),
            vmem((128, width), BF16),
            vmem((128, width), BF16),
            vmem((2, 4 * nproj, nhigh), F32),
            vmem((4 * nproj, 128), F32),
            vmem((npw, 8, 128), F32),
            vmem((2, 3 * nocc, 256), BF16),
            vmem((2, 3, nocc, nhigh), F32),
            vmem((half, 2, 48, nhigh), BF16),
            vmem((half, 2, 48, nhigh), BF16),
            vmem((nz, 8, 128), F32),
            vmem((half, 56, nhigh), F32),
            vmem((half, 56, nhigh), F32),
            vmem((half - 1, 56, nhigh), F32),
            vmem((half - 1, 56, nhigh), F32),
            vmem((half, 2, 48, nhigh), BF16),
            vmem((half, 2, 48, nhigh), BF16),
            vmem((half, 48, nhigh), F32),
            vmem((half, 48, nhigh), F32),
            vmem((half - 1, 48, nhigh), F32),
            vmem((half - 1, 48, nhigh), F32),
            vmem((8, 128), F32),
            vmem((nband, 8, 128), F32),
            dma((nband - 1,)),
            dma((nband,)),
            dma((half,)),
            dma((half,)),
            dma((1,)),
            dma((1,)),
            dma((half,)),
            dma((half,)),
            dma((half - 1,)),
            dma((half - 1,)),
            dma((half,)),
            dma((half,)),
            dma((half,)),
            dma((half,)),
            dma((half - 1,)),
            dma((half - 1,)),
            dma((nband - 1,)),
            dma((nband,)),
        ],
        compiler_params=pltpu.CompilerParams(
            collective_id=0, has_side_effects=True, vmem_limit_bytes=52 * 1024 * 1024
        ),
    )(psi_occ, psi_high, miller, table, strength, recip, kfrac)
    return out


def solution(mesh):
    nz = mesh.shape["pw"] // 2
    nx = mesh.shape["band"] // 4
    placed = (
        P(None, "band", "pw"),
        P(None, "band", "pw"),
        P(None, "pw"),
        P(),
        P(),
        P(),
        P(),
        P(),
        P(),
        P(),
    )
    return jax.shard_map(
        functools.partial(on_device, nz, nx),
        mesh=mesh,
        in_specs=placed,
        out_specs=P(None, None, "pw", "band"),
        check_vma=False,
    )
```

time: 406 us -> 104 us (0.26)
  the two profiles are of different devices: /device:TPU:1 before, /device:TPU:8 now
where the time goes in v1:
time: 104 us; the launch traced here: 103 us
  Pallas kernels  97.5 us (94%)
  local copies, waits for them, and re-layouts  4.12 us (4%)
  matrix products  1.8 us (2%)
    pallas_call x1, Pallas kernels, on_device(): pl.pallas_call(functools.partial(kernel, nz, nx), out_shape=jax.ShapeDtyp...  97.5 us
    unnamed x9, local copies, waits for them, and re-layouts  3.59 us

profile of v1, /device:TPU:8, one launch (start us, length us, event | category | flops | bytes accessed | tf_op | source)
XLA Modules:
  0.0 103.5 jit_solution(9536850083660355477)
XLA Ops:
  0.0 0.9 fusion.2
  0.9 0.9 fusion
  1.8 0.2 copy.12.par_ref
  2.0 0.1 broadcast_in_dim.6
  2.1 0.1 broadcast_in_dim.7
  2.2 0.2 broadcast_in_dim.16.strength_ref
  2.4 0.0 copy-start
  2.4 0.9 copy-done
  3.3 0.0 copy-start.1
  3.3 0.7 copy-done.1
  4.0 0.0 copy-start.2
  4.0 0.7 copy-done.2
  4.7 0.0 copy-start.3
  4.7 0.7 copy-done.3
  5.4 97.5 %shard_map.100 = f32[3,2,8,256]{3,2,1,0:T(8,128)S(1)} custom-call(bf16[2,16,1536]{2,1,0:T(8,128)(2,1)S(1)} %copy-done, bf16[2,256,1536]{2,1,0:T(8,128)(2,1)} %high_ref.1, s32[3,1536]{1,0:T(4,128)S(1)} %copy-done.1, f32[192,5]{1,0:T(8,128)S(1)} %copy.12.par_ref, f32[768,128]{1,0:T(8,128)S(1)} %broadcast_in_dim.16.strength_ref, f32[3,3]{1,0:T(4,128)S(1)} %copy-done.2, ...), custom_call_target="tpu_custom_call" | custom-call | tf_op jit(solution)/shard_map/pallas_call | solution.py:443
  102.8 0.6 copy.14
  (1 shorter events, 0.0 us)
Async XLA Ops:
  2.4 0.9 copy-start
  3.3 0.7 copy-start.1
  4.0 0.7 copy-start.2
  4.7 0.7 copy-start.3

commit v2 on v1

--- a/solution.py
+++ b/solution.py
@@ -11,6 +11,10 @@
 F32 = jnp.float32
 BF16 = jnp.bfloat16
 LANES = 512
+MOVES = [(8, 4), (-7, -3), (7, 3), (-6, -2), (6, 2), (-5, -1), (5, 1)]
+RELAYS = [4, -4]
+DIRECT = [3, -3, 2, -2, 1, -1]
+ORDER = [offset for offset, _ in MOVES] + RELAYS + DIRECT + [0]
 
 
 def projector_table(positions, atom_type, proj_atom, widths, dion):
@@ -76,16 +80,14 @@
     ys1,
     yr1,
     oyr,
-    us1,
-    ur1,
-    ds1,
-    dr1,
+    zs1,
+    zr1,
     ys2,
     yr2,
-    us2,
-    ur2,
-    ds2,
-    dr2,
+    zs2,
+    zr2,
+    tile_send,
+    tile_recv,
     tile_own,
     tiles,
     g_send,
@@ -94,16 +96,14 @@
     y1_recv,
     oy_send,
     oy_recv,
-    u1_send,
-    u1_recv,
-    d1_send,
-    d1_recv,
+    ts_send,
+    ts_recv,
+    z1_send,
+    z1_recv,
     y2_send,
     y2_recv,
-    u2_send,
-    u2_recv,
-    d2_send,
-    d2_recv,
+    z2_send,
+    z2_recv,
     t_send,
     t_recv,
 ):
@@ -112,7 +112,6 @@
     nband = 4 * nx
     y_lo, z = p // nz, p % nz
     y_hi, x, core = b // (2 * nx), (b // 2) % nx, b % 2
-    half = nz // 2
     width = high_ref.shape[2]
 
     def band_id(yy, xx, cc):
@@ -132,40 +131,21 @@
         )
 
     y_mate = pw_id(1 - y_lo, z)
-    z_up = pw_id(y_lo, (z + 1) % nz)
-    z_down = pw_id(y_lo, (z + nz - 1) % nz)
+
+    def z_at(offset):
+        return pw_id(y_lo, (z + offset + nz) % nz)
+
 
     barrier = pltpu.get_barrier_semaphore()
-    for pw in (y_mate, z_up, z_down):
-        pl.semaphore_signal(barrier, inc=1, device_id={"pw": pw, "band": b}, device_id_type=MESH)
+    pl.semaphore_signal(barrier, inc=1, device_id={"pw": y_mate, "band": b}, device_id_type=MESH)
+    for step in range(1, nz):
+        pl.semaphore_signal(
+            barrier, inc=1, device_id={"pw": z_at(step), "band": b}, device_id_type=MESH
+        )
     for step in range(1, nband):
         pl.semaphore_signal(
             barrier, inc=1, device_id={"pw": p, "band": (b + step) % nband}, device_id_type=MESH
         )
-    pl.semaphore_wait(barrier, 3 + nband - 1)
-
-    started = []
-
-    def forward(src, block, count, bands):
-        for band in bands:
-            copy = put(src, occ_all.at[block], g_send.at[count], g_recv.at[block], p, band)
-            copy.start()
-            started.append(copy)
-            count += 1
-        return count
-
-    def block_arrived(block):
-        put(occ_all.at[block], occ_all.at[block], g_send.at[0], g_recv.at[block], p, b).wait_recv()
-
-    mate_block = band_id(1 - y_hi, x, core)
-    x_others = [(x + dx) % nx for dx in range(1, nx)]
-    sent = forward(
-        occ_ref,
-        b,
-        0,
-        [mate_block] + [band_id(y_hi, xx, core) for xx in x_others] + [band_id(y_hi, x, 1 - core)],
-    )
-    occ_all[b] = occ_ref[...]
 
     shifted = [miller_ref[axis : axis + 1, :].astype(F32) + kfrac_ref[axis] for axis in range(3)]
     vectors = [
@@ -218,6 +198,52 @@
 
     lax.fori_loop(0, (par_ref.shape[0] // 8) * pieces, build, 0)
 
+    pl.semaphore_wait(barrier, nz + nband - 1)
+
+    started = []
+
+    def forward(src, block, count, bands):
+        for band in bands:
+            copy = put(src, occ_all.at[block], g_send.at[count], g_recv.at[block], p, band)
+            copy.start()
+            started.append(copy)
+            count += 1
+        return count
+
+    def block_arrived(block):
+        put(occ_all.at[block], occ_all.at[block], g_send.at[0], g_recv.at[block], p, b).wait_recv()
+
+    mate_block = band_id(1 - y_hi, x, core)
+    x_others = [(x + dx) % nx for dx in range(1, nx)]
+    sent = forward(
+        occ_ref,
+        b,
+        0,
+        [mate_block] + [band_id(y_hi, xx, core) for xx in x_others] + [band_id(y_hi, x, 1 - core)],
+    )
+    occ_all[b] = occ_ref[...]
+
+    coef[...] = jnp.zeros_like(coef)
+    occ_coef[...] = jnp.zeros_like(occ_coef)
+
+    def project_occ(index, carry):
+        columns = pl.ds(pl.multiple_of(index * 256, 256), 256)
+        occ_coef[...] += dot_t(proj[0, :, columns], occ_a[:, columns]) + dot_t(
+            proj[1, :, columns], occ_b[:, columns]
+        )
+        return carry
+
+    lax.fori_loop(0, width // 256, project_occ, 0)
+    npw = 2 * nz
+    for owner in range(npw):
+        rows = occ_coef[24 * owner : 24 * owner + 24, :] * strength_ref[24 * owner : 24 * owner + 24, :]
+        occ_tile[owner] = (
+            rows[0:8] + pltpu.roll(rows[8:16], 32, 1) + pltpu.roll(rows[16:24], 64, 1)
+        )
+    tile_copy = put(
+        occ_tile.at[pl.ds((1 - y_lo) * nz, nz)], oyr, oy_send.at[0], oy_recv.at[0], y_mate, b
+    )
+    tile_copy.start()
     block_arrived(mate_block)
     sent = forward(
         occ_all.at[mate_block],
@@ -226,108 +252,84 @@
         [band_id(y_hi, xx, core) for xx in x_others] + [band_id(y_hi, x, 1 - core)],
     )
 
-    coef[...] = jnp.zeros_like(coef)
-    occ_coef[...] = jnp.zeros_like(occ_coef)
-
     def project(index, carry):
         columns = pl.ds(pl.multiple_of(index * 256, 256), 256)
         real, imag = proj[0, :, columns], proj[1, :, columns]
         high_r, high_i = high_ref[0, :, columns], high_ref[1, :, columns]
-        occ_coef[...] += dot_t(real, occ_a[:, columns]) + dot_t(imag, occ_b[:, columns])
         coef[0] += dot_t(real, high_r) + dot_t(imag, high_i)
         coef[1] += dot_t(real, high_i) - dot_t(imag, high_r)
         return carry
 
     lax.fori_loop(0, width // 256, project, 0)
 
-    npw = 2 * nz
-    for owner in range(npw):
-        rows = occ_coef[24 * owner : 24 * owner + 24, :] * strength_ref[24 * owner : 24 * owner + 24, :]
-        occ_tile[owner] = (
-            rows[0:8] + pltpu.roll(rows[8:16], 32, 1) + pltpu.roll(rows[16:24], 64, 1)
-        )
-
     def chunk1(owner):
         return coef[:, pl.ds(pl.multiple_of(owner * 24, 8), 24), :].reshape(48, 256)
 
     def chunk2(owner):
         return total[:, :, pl.ds(pl.multiple_of(owner * 8, 8), 8), :].reshape(48, 256)
 
-    def up_dest(step):
-        return (z + half - step + nz) % nz
-
-    def down_dest(step):
-        return (z + half + 1 + step) % nz
-
     def mate_sends(chunk, ys, yr, send, recv):
         copies = []
-        for step in range(half):
-            ys[step, 0] = chunk(pw_id(1 - y_lo, up_dest(step))).astype(BF16)
-            ys[step, 1] = chunk(pw_id(1 - y_lo, down_dest(step))).astype(BF16)
-            copy = put(ys.at[step], yr.at[step], send.at[step], recv.at[step], y_mate, b)
+        for place, offset in enumerate(ORDER):
+            ys[place] = chunk(pw_id(1 - y_lo, (z + offset + nz) % nz)).astype(BF16)
+            copy = put(ys.at[place], yr.at[place], send.at[place], recv.at[place], y_mate, b)
             copy.start()
             copies.append(copy)
         return copies
 
-    tile_copy = put(
-        occ_tile.at[pl.ds((1 - y_lo) * nz, nz)], oyr, oy_send.at[0], oy_recv.at[0], y_mate, b
-    )
-    tile_copy.start()
+    def reduce_z(chunk, mates, yr, zs, zr, send, recv, fill):
+        copies = {}
+
+        def local(offset):
+            place = ORDER.index(offset)
+            mates[place].wait_recv()
+            return chunk(z_at(offset)) + yr[place].astype(F32)
+
+        def push(slot, value, offset):
+            zs[slot] = value.astype(BF16)
+            copy = put(zs.at[slot], zr.at[slot], send.at[slot], recv.at[slot], z_at(offset), b)
+            copy.start()
+            copies[slot] = copy
+
+        def arrived(slot):
+            copies[slot].wait_recv()
+            return zr[slot].astype(F32)
+
+        for slot, (offset, target) in enumerate(MOVES):
+            push(slot, local(offset), target)
+        relayed = [local(offset) for offset in RELAYS]
+        for place, offset in enumerate(DIRECT):
+            push(len(MOVES) + place, local(offset), offset)
+        fill(0)
+        for place, offset in enumerate(RELAYS):
+            value = relayed[place]
+            for slot, (_, target) in enumerate(MOVES):
+                if target * offset > 0:
+                    value = value + arrived(slot)
+            push(len(MOVES) + len(DIRECT) + place, value, offset)
+        fill(1)
+        value = local(0)
+        for place in range(len(DIRECT) + len(RELAYS)):
+            value = value + arrived(len(MOVES) + place)
+        return value, list(copies.values())
+
     mates1 = mate_sends(chunk1, ys1, yr1, y1_send, y1_recv)
-
-    def occ_sum(dest):
-        tile = occ_tile[pw_id(y_lo, dest)] + oyr[dest]
-        return jnp.concatenate([tile, jnp.zeros_like(tile)], axis=1)
-
+    tile_copy.wait_recv()
+    spread_copies = []
+    for step in range(1, nz):
+        dest = (z + step) % nz
+        tile_send[step] = occ_tile[pw_id(y_lo, dest)] + oyr[dest]
+        copy = put(
+            tile_send.at[step], tile_recv.at[step], ts_send.at[step], ts_recv.at[step], z_at(step), b
+        )
+        copy.start()
+        spread_copies.append(copy)
     for yy in (y_hi, 1 - y_hi):
         for xx in x_others:
             block = band_id(yy, xx, core)
             block_arrived(block)
             sent = forward(occ_all.at[block], block, sent, [band_id(y_hi, x, 1 - core)])
-    tile_copy.wait_recv()
     total[...] = jnp.zeros_like(total)
-
-    rings = []
-
-    def ring_step(step, chunk, yr, mates, us, ur, ds, dr, u_send, u_recv, d_send, d_recv, tail):
-        mates[step].wait_recv()
-        if step > 0:
-            rings_up[step - 1].wait_recv()
-        dest = up_dest(step)
-        value = chunk(pw_id(y_lo, dest)) + yr[step, 0].astype(F32)
-        if step > 0:
-            value = value + ur[step - 1, 0:48, :]
-        us[step, 0:48, :] = value
-        if tail:
-            extra = occ_sum(dest)
-            if step > 0:
-                extra = extra + ur[step - 1, 48:56, :]
-            us[step, 48:56, :] = extra
-        copy = put(us.at[step], ur.at[step], u_send.at[step], u_recv.at[step], z_up, b)
-        copy.start()
-        rings_up.append(copy)
-        if step < half - 1:
-            if step > 0:
-                rings_down[step - 1].wait_recv()
-            dest = down_dest(step)
-            value = chunk(pw_id(y_lo, dest)) + yr[step, 1].astype(F32)
-            if step > 0:
-                value = value + dr[step - 1, 0:48, :]
-            ds[step, 0:48, :] = value
-            if tail:
-                extra = occ_sum(dest)
-                if step > 0:
-                    extra = extra + dr[step - 1, 48:56, :]
-                ds[step, 48:56, :] = extra
-            copy = put(ds.at[step], dr.at[step], d_send.at[step], d_recv.at[step], z_down, b)
-            copy.start()
-            rings_down.append(copy)
-
-    def ring_end(chunk, yr, ur, dr):
-        rings_up[half - 1].wait_recv()
-        rings_down[half - 2].wait_recv()
-        value = chunk(pw_id(y_lo, z)) + yr[half - 1, 1].astype(F32)
-        return value + ur[half - 1, 0:48, :] + dr[half - 2, 0:48, :]
 
     nocc = total.shape[2]
 
@@ -343,32 +345,33 @@
         total[0] += (dot_t(real, high_r) + dot_t(imag, high_i)).reshape(3, nocc, 256)
         total[1] += (dot_t(real, high_i) - dot_t(imag, high_r)).reshape(3, nocc, 256)
 
-    rings_up, rings_down = [], []
-    ring_refs = (us1, ur1, ds1, dr1, u1_send, u1_recv, d1_send, d1_recv)
-    ring_step(0, chunk1, yr1, mates1, *ring_refs, True)
-    for xx in [x] + x_others:
-        for yy in range(2):
-            block_arrived(band_id(yy, xx, 1 - core))
-    for step in range(1, half):
-        ring_step(step, chunk1, yr1, mates1, *ring_refs, True)
-        if step - 1 < width // 256:
-            momentum_piece(step - 1)
-    for index in range(half - 1, width // 256):
-        momentum_piece(index)
-    high_sum = ring_end(chunk1, yr1, ur1, dr1)
-    tile_own[...] = (
-        occ_tile[p] + oyr[z] + ur1[half - 1, 48:56, 0:128] + dr1[half - 2, 48:56, 0:128]
-    )
-    rings1 = rings_up + rings_down
-
     tile_copies = []
-    for step in range(1, nband):
-        copy = put(
-            tile_own, tiles.at[b], t_send.at[step - 1], t_recv.at[b], p, (b + step) % nband
-        )
-        copy.start()
-        tile_copies.append(copy)
-    tiles[b] = tile_own[...]
+
+    def fill1(point):
+        if point == 0:
+            tile = occ_tile[p] + oyr[z]
+            for copy, step in zip(spread_copies, range(1, nz)):
+                copy.wait_recv()
+                tile = tile + tile_recv[step]
+            tile_own[...] = tile
+            for step in range(1, nband):
+                copy = put(
+                    tile_own, tiles.at[b], t_send.at[step - 1], t_recv.at[b], p, (b + step) % nband
+                )
+                copy.start()
+                tile_copies.append(copy)
+            tiles[b] = tile
+            for xx in [x] + x_others:
+                for yy in range(2):
+                    block_arrived(band_id(yy, xx, 1 - core))
+            momentum_piece(0)
+            momentum_piece(1)
+        else:
+            for index in range(2, width // 256):
+                momentum_piece(index)
+
+    high_sum, moves1 = reduce_z(chunk1, mates1, yr1, zs1, zr1, z1_send, z1_recv, fill1)
+
     high_hi = high_sum.astype(BF16)
     high_lo = (high_sum - high_hi.astype(F32)).astype(BF16)
     rhs = jnp.concatenate([high_hi, high_lo, high_hi], axis=0)
@@ -416,16 +419,17 @@
             )
 
     mates2 = mate_sends(chunk2, ys2, yr2, y2_send, y2_recv)
-    rings_up, rings_down = [], []
-    ring_refs = (us2, ur2, ds2, dr2, u2_send, u2_recv, d2_send, d2_recv)
-    for step in range(half):
-        ring_step(step, chunk2, yr2, mates2, *ring_refs, False)
-    result = ring_end(chunk2, yr2, ur2, dr2).reshape(2, 3, 8, 256)
+    result, moves2 = reduce_z(
+        chunk2, mates2, yr2, zs2, zr2, z2_send, z2_recv, lambda point: None
+    )
+    result = result.reshape(2, 3, 8, 256)
     for axis in range(3):
         for part in range(2):
             out_ref[axis, part] = result[part, axis]
 
-    for copy in started + [tile_copy] + mates1 + rings1 + tile_copies + mates2 + rings_up + rings_down:
+    for copy in (
+        started + [tile_copy] + mates1 + spread_copies + moves1 + tile_copies + mates2 + moves2
+    ):
         copy.wait_send()
 
 
@@ -434,7 +438,7 @@
 ):
     nproj = proj_atom.shape[0]
     nown, nhigh, width = psi_occ.shape[1], psi_high.shape[1], psi_high.shape[2]
-    npw, nband, half = 2 * nz, 4 * nx, nz // 2
+    npw, nband = 2 * nz, 4 * nx
     nocc = nown * nband
     table = projector_table(positions, atom_type, proj_atom, widths, dion)
     strength = jnp.broadcast_to(jnp.repeat(table[:, 4:5], 4, axis=0), (4 * nproj, 128))
@@ -457,37 +461,33 @@
             vmem((npw, 8, 128), F32),
             vmem((2, 3 * nocc, 256), BF16),
             vmem((2, 3, nocc, nhigh), F32),
-            vmem((half, 2, 48, nhigh), BF16),
-            vmem((half, 2, 48, nhigh), BF16),
+            vmem((nz, 48, nhigh), BF16),
+            vmem((nz, 48, nhigh), BF16),
             vmem((nz, 8, 128), F32),
-            vmem((half, 56, nhigh), F32),
-            vmem((half, 56, nhigh), F32),
-            vmem((half - 1, 56, nhigh), F32),
-            vmem((half - 1, 56, nhigh), F32),
-            vmem((half, 2, 48, nhigh), BF16),
-            vmem((half, 2, 48, nhigh), BF16),
-            vmem((half, 48, nhigh), F32),
-            vmem((half, 48, nhigh), F32),
-            vmem((half - 1, 48, nhigh), F32),
-            vmem((half - 1, 48, nhigh), F32),
+            vmem((nz - 1, 48, nhigh), BF16),
+            vmem((nz - 1, 48, nhigh), BF16),
+            vmem((nz, 48, nhigh), BF16),
+            vmem((nz, 48, nhigh), BF16),
+            vmem((nz - 1, 48, nhigh), BF16),
+            vmem((nz - 1, 48, nhigh), BF16),
+            vmem((nz, 8, 128), F32),
+            vmem((nz, 8, 128), F32),
             vmem((8, 128), F32),
             vmem((nband, 8, 128), F32),
             dma((nband - 1,)),
             dma((nband,)),
-            dma((half,)),
-            dma((half,)),
+            dma((nz,)),
+            dma((nz,)),
             dma((1,)),
             dma((1,)),
-            dma((half,)),
-            dma((half,)),
-            dma((half - 1,)),
-            dma((half - 1,)),
-            dma((half,)),
-            dma((half,)),
-            dma((half,)),
-            dma((half,)),
-            dma((half - 1,)),
-            dma((half - 1,)),
+            dma((nz,)),
+            dma((nz,)),
+            dma((nz - 1,)),
+            dma((nz - 1,)),
+            dma((nz,)),
+            dma((nz,)),
+            dma((nz - 1,)),
+            dma((nz - 1,)),
             dma((nband - 1,)),
             dma((nband,)),
         ],

time: 104 us -> 71.4 us (0.69)
  the two profiles are of different devices: /device:TPU:8 before, /device:TPU:2 now
where the time goes in v2:
time: 71.4 us; the launch traced here: 71.1 us
  Pallas kernels  65.1 us (91%)
  local copies, waits for them, and re-layouts  4.12 us (6%)
  matrix products  1.8 us (3%)
    pallas_call x1, Pallas kernels, on_device(): pl.pallas_call(functools.partial(kernel, nz, nx), out_shape=jax.ShapeDtyp...  65.1 us
    unnamed x9, local copies, waits for them, and re-layouts  3.59 us

profile of v2, /device:TPU:2, one launch (start us, length us, event | category | flops | bytes accessed | tf_op | source)
XLA Modules:
  0.0 71.1 jit_solution(6320613622817405157)
XLA Ops:
  0.0 0.9 %fusion.2 = f32[48,2]{0,1:T(2,128)S(1)} fusion(s32[48]{0:T(128)} %param.16, f32[3,1]{0,1:T(1,128)} %bitcast.4, f32[3,1]{0,1:T(1,128)} %bitcast.5), kind=kOutput, calls=%fused_computation.4 | convolution fusion | flops 3606 | bytes 600 | tf_op jit(solution)/shard_map/dot_general | solution.py:27
  0.9 0.9 %fusion = f32[192,5]{0,1:T(8,128)S(1)} fusion(s32[192]{0:T(256)} %param.17, f32[48,2]{0,1:T(2,128)S(1)} %fusion.2, f32[48,3]{0,1:T(4,128)} %param.15), kind=kOutput, calls=%fused_computation.1 | convolution fusion | flops 562416 | bytes 5568 | tf_op jit(solution)/shard_map/dot_general | solution.py:28
  1.8 0.2 copy.12.par_ref
  2.0 0.1 broadcast_in_dim.6
  2.1 0.1 broadcast_in_dim.7
  2.2 0.2 broadcast_in_dim.16.strength_ref
  2.4 0.0 copy-start
  2.4 0.9 %copy-done = bf16[2,16,1536]{2,1,0:T(8,128)(2,1)S(1)} copy-done((bf16[2,16,1536]{2,1,0:T(8,128)(2,1)S(1)}, bf16[2,16,1536]{2,1,0:T(8,128)(2,1)}, u32[]{:S(2)}) %copy-start) | copy-done | bytes 98328
  3.3 0.0 copy-start.1
  3.3 0.7 %copy-done.1 = s32[3,1536]{1,0:T(4,128)S(1)} copy-done((s32[3,1536]{1,0:T(4,128)S(1)}, s32[3,1536]{1,0:T(4,128)}, u32[]{:S(2)}) %copy-start.1) | copy-done | bytes 18456
  4.0 0.0 copy-start.2
  4.0 0.7 copy-done.2
  4.7 0.0 copy-start.3
  4.7 0.7 copy-done.3
  5.4 65.1 %shard_map.100 = f32[3,2,8,256]{3,2,1,0:T(8,128)S(1)} custom-call(bf16[2,16,1536]{2,1,0:T(8,128)(2,1)S(1)} %copy-done, bf16[2,256,1536]{2,1,0:T(8,128)(2,1)} %high_ref.1, s32[3,1536]{1,0:T(4,128)S(1)} %copy-done.1, f32[192,5]{1,0:T(8,128)S(1)} %copy.12.par_ref, f32[768,128]{1,0:T(8,128)S(1)} %broadcast_in_dim.16.strength_ref, f32[3,3]{1,0:T(4,128)S(1)} %copy-done.2, ...), custom_call_target="tpu_custom_call" | custom-call | tf_op jit(solution)/shard_map/pallas_call | solution.py:447
  70.5 0.6 copy.14
  (1 shorter events, 0.0 us)
Async XLA Ops:
  2.4 0.9 %copy-start = (bf16[2,16,1536]{2,1,0:T(8,128)(2,1)S(1)}, bf16[2,16,1536]{2,1,0:T(8,128)(2,1)}, u32[]{:S(2)}) copy-start(bf16[2,16,1536]{2,1,0:T(8,128)(2,1)} %occ_ref.1) | copy-start | bytes 294916
  3.3 0.7 %copy-start.1 = (s32[3,1536]{1,0:T(4,128)S(1)}, s32[3,1536]{1,0:T(4,128)}, u32[]{:S(2)}) copy-start(s32[3,1536]{1,0:T(4,128)} %miller_ref.1) | copy-start | bytes 55300
  4.0 0.7 copy-start.2
  4.7 0.7 copy-start.3

commit v3 on v2

--- a/solution.py
+++ b/solution.py
@@ -17,17 +17,6 @@
 ORDER = [offset for offset, _ in MOVES] + RELAYS + DIRECT + [0]
 
 
-def projector_table(positions, atom_type, proj_atom, widths, dion):
-    hp = lax.Precision.HIGHEST
-    atom_hot = (
-        proj_atom[:, None] == jnp.arange(positions.shape[0], dtype=jnp.int32)[None, :]
-    ).astype(F32)
-    type_hot = (atom_type[:, None] == jnp.arange(widths.shape[0], dtype=jnp.int32)[None, :]).astype(F32)
-    per_type = jnp.stack([widths, dion], axis=1)
-    per_atom = jnp.concatenate([positions, jnp.dot(type_hot, per_type, precision=hp)], axis=1)
-    return jnp.dot(atom_hot, per_atom, precision=hp)
-
-
 def sin_cos(angle):
     turns = jnp.floor(angle * 0.6366197723675814 + 0.5)
     rest = angle - turns * 1.5703125
@@ -58,18 +47,37 @@
 def kernel(
     nz,
     nx,
-    occ_ref,
+    occ_hbm,
+    high_hbm,
+    miller_hbm,
+    recip_hbm,
+    kfrac_hbm,
+    positions_hbm,
+    atom_type_hbm,
+    proj_atom_hbm,
+    widths_hbm,
+    dion_hbm,
+    out_ref,
     high_ref,
     miller_ref,
-    par_ref,
-    strength_ref,
     recip_ref,
     kfrac_ref,
-    out_ref,
+    positions_ref,
+    atom_type_ref,
+    proj_atom_ref,
+    widths_ref,
+    dion_ref,
+    in_sem,
     occ_all,
     wave,
-    stage,
+    waves,
+    radial,
+    pick_cos,
+    pick_sin,
+    type_hot,
+    strength_ref,
     proj,
+    lefts,
     occ_a,
     occ_b,
     coef,
@@ -112,7 +120,7 @@
     nband = 4 * nx
     y_lo, z = p // nz, p % nz
     y_hi, x, core = b // (2 * nx), (b // 2) % nx, b % 2
-    width = high_ref.shape[2]
+    width, nown = high_hbm.shape[2], occ_hbm.shape[1]
 
     def band_id(yy, xx, cc):
         return yy * (2 * nx) + xx * 2 + cc
@@ -136,6 +144,23 @@
         return pw_id(y_lo, (z + offset + nz) % nz)
 
 
+    sources = (
+        (occ_hbm, occ_all.at[b]),
+        (high_hbm, high_ref),
+        (miller_hbm, miller_ref),
+        (recip_hbm, recip_ref),
+        (kfrac_hbm, kfrac_ref),
+        (positions_hbm, positions_ref),
+        (atom_type_hbm, atom_type_ref),
+        (proj_atom_hbm, proj_atom_ref),
+        (widths_hbm, widths_ref),
+        (dion_hbm, dion_ref),
+    )
+    loads = [
+        pltpu.make_async_copy(src, dst, in_sem.at[place]) for place, (src, dst) in enumerate(sources)
+    ]
+    for copy in loads[2:] + loads[:2]:
+        copy.start()
     barrier = pltpu.get_barrier_semaphore()
     pl.semaphore_signal(barrier, inc=1, device_id={"pw": y_mate, "band": b}, device_id_type=MESH)
     for step in range(1, nz):
@@ -147,9 +172,15 @@
             barrier, inc=1, device_id={"pw": p, "band": (b + step) % nband}, device_id_type=MESH
         )
 
-    shifted = [miller_ref[axis : axis + 1, :].astype(F32) + kfrac_ref[axis] for axis in range(3)]
+    for copy in loads[2:]:
+        copy.wait()
+    shifted = [
+        miller_ref[axis : axis + 1, :].astype(F32) + kfrac_ref[0:1, axis : axis + 1] for axis in range(3)
+    ]
     vectors = [
-        shifted[0] * recip_ref[0, axis] + shifted[1] * recip_ref[1, axis] + shifted[2] * recip_ref[2, axis]
+        shifted[0] * recip_ref[0:1, axis : axis + 1]
+        + shifted[1] * recip_ref[1:2, axis : axis + 1]
+        + shifted[2] * recip_ref[2:3, axis : axis + 1]
         for axis in range(3)
     ]
     for axis in range(3):
@@ -157,47 +188,92 @@
     wave[3] = jnp.broadcast_to(
         vectors[0] * vectors[0] + vectors[1] * vectors[1] + vectors[2] * vectors[2], (8, width)
     )
-    nown = occ_ref.shape[1]
-    occ_a[...] = jnp.zeros_like(occ_a)
-    occ_b[...] = jnp.zeros_like(occ_b)
-    occ_a[0:nown, :] = occ_ref[0]
-    occ_a[nown : 2 * nown, :] = occ_ref[1]
-    occ_b[0:nown, :] = occ_ref[1]
-    occ_b[nown : 2 * nown, :] = -occ_ref[0]
-
-    channel = lax.broadcasted_iota(jnp.int32, (8, LANES), 0) % 4
-    selectors = [(channel == value).astype(F32) for value in range(4)]
-    pieces = width // LANES
-
-    def place(part, kind, value):
-        for piece in range(LANES // 128):
-            stage[part, piece, pl.ds(kind, 8, stride=4), :] = value[:, 128 * piece : 128 * piece + 128]
-
-    def build(index, carry):
-        block = index // pieces
-        columns = pl.ds(pl.multiple_of((index % pieces) * LANES, LANES), LANES)
-        table = par_ref[pl.ds(pl.multiple_of(block * 8, 8), 8), :]
-        k = [wave[axis, :, columns] for axis in range(3)]
-        square = wave[3, :, columns]
-        spread = table[:, 3:4]
-        envelope = jnp.exp(-0.5 * spread * square)
-        angular = selectors[0] + selectors[1] * k[0] + selectors[2] * k[1] + selectors[3] * k[2]
-        sine, cosine = sin_cos(table[:, 0:1] * k[0] + table[:, 1:2] * k[1] + table[:, 2:3] * k[2])
-        radial = envelope * angular
-        place(0, 0, radial * cosine)
-        place(1, 0, -radial * sine)
-        for axis in range(3):
-            factor = envelope * (selectors[axis + 1] - spread * k[axis] * angular)
-            place(0, axis + 1, factor * sine)
-            place(1, axis + 1, factor * cosine)
-        rows = pl.ds(pl.multiple_of(block * 32, 32), 32)
-        for part in range(2):
-            pieces_of = [stage[part, piece] for piece in range(LANES // 128)]
-            proj[part, rows, columns] = jnp.concatenate(pieces_of, axis=1).astype(BF16)
+
+    nproj, natom, ntype = proj_atom_ref.shape[1], atom_type_ref.shape[1], widths_ref.shape[1]
+    nrow = 4 * nproj
+    atoms = lax.rem(lax.broadcasted_iota(jnp.int32, (4 * natom, nproj), 0), natom)
+    atom_hot = (atoms == proj_atom_ref[...]).astype(F32).astype(BF16)
+    row_of = lax.broadcasted_iota(jnp.int32, (nrow, nproj), 0) // 4
+    row_hot = (row_of == lax.broadcasted_iota(jnp.int32, (nrow, nproj), 1)).astype(F32).astype(BF16)
+    hot = dot_t(row_hot, atom_hot)
+    types = lax.broadcasted_iota(jnp.int32, (8, natom), 0)
+    of_type = (types == atom_type_ref[...]).astype(F32)
+    by_type = dot_t(hot[:, 0:natom].astype(BF16), of_type.astype(BF16))
+    type_hot[...] = by_type
+    weight = by_type[:, 0:1] * dion_ref[0:1, 0:1]
+    for value in range(1, ntype):
+        weight = weight + by_type[:, value : value + 1] * dion_ref[0:1, value : value + 1]
+    strength_ref[...] = jnp.broadcast_to(weight, (nrow, 128))
+    is_value = lax.rem(lax.broadcasted_iota(jnp.int32, (nrow, 4 * natom), 0), 4) == 0
+    in_cos = lax.broadcasted_iota(jnp.int32, (nrow, 4 * natom), 1) < 2 * natom
+    zero = jnp.zeros_like(hot)
+    pick_cos[...] = jnp.where(is_value == in_cos, hot, zero).astype(BF16)
+    pick_sin[...] = jnp.where(is_value, jnp.where(in_cos, zero, -hot), jnp.where(in_cos, hot, zero)).astype(
+        BF16
+    )
+
+    centers = positions_ref[...].T
+    row = lax.broadcasted_iota(jnp.int32, (8, LANES), 0)
+
+    def tables(index, carry):
+        columns = pl.ds(pl.multiple_of(index * LANES, LANES), LANES)
+        k = [wave[axis, :, columns] for axis in range(4)]
+        for first in range(0, natom, 16):
+            parts = []
+            for begin in (first, first + 8):
+                place = centers[begin : begin + 8]
+                parts.append(sin_cos(place[:, 0:1] * k[0] + place[:, 1:2] * k[1] + place[:, 2:3] * k[2]))
+            for block, which in ((0, 1), (2, 0)):
+                value = jnp.concatenate([parts[0][which], parts[1][which]], axis=0)
+                upper = value.astype(BF16)
+                waves[block * natom + first : block * natom + first + 16, columns] = upper
+                waves[(block + 1) * natom + first : (block + 1) * natom + first + 16, columns] = (
+                    value - upper.astype(F32)
+                ).astype(BF16)
+        kind = lax.rem(row, 4)
+        along = jnp.where(kind == 1, k[0], jnp.where(kind == 2, k[1], k[2]))
+        for value in range(ntype):
+            spread = widths_ref[0:1, value : value + 1]
+            envelope = jnp.exp(-0.5 * spread * k[3])
+            for pair in range(2):
+                channel = 2 * pair + row // 4
+                if pair == 0:
+                    angular = jnp.where(channel == 0, jnp.ones_like(along), k[0])
+                else:
+                    angular = jnp.where(channel == 2, k[1], k[2])
+                matching = ((channel == kind) & (kind > 0)).astype(F32)
+                factor = jnp.where(kind == 0, angular, matching - spread * along * angular)
+                radial[value, 8 * pair : 8 * pair + 8, columns] = envelope * factor
         return carry
 
-    lax.fori_loop(0, (par_ref.shape[0] // 8) * pieces, build, 0)
-
+    lax.fori_loop(0, width // LANES, tables, 0)
+
+    hrow = nrow // 2
+
+    def build(half):
+        rows = pl.ds(pl.multiple_of(half * hrow, hrow), hrow)
+        left_cos, left_sin = pick_cos[rows, :], pick_sin[rows, :]
+        kinds = type_hot[rows, :]
+
+        def tile(index, carry):
+            columns = pl.ds(pl.multiple_of(index * 256, 256), 256)
+            right = waves[:, columns]
+            table = [
+                jnp.broadcast_to(radial[value, :, columns][None], (hrow // 16, 16, 256)).reshape(hrow, 256)
+                for value in range(ntype)
+            ]
+            part = table[0]
+            for value in range(1, ntype):
+                part = jnp.where(kinds[:, value : value + 1] > 0.5, table[value], part)
+            proj[0, rows, columns] = (part * jnp.dot(left_cos, right, preferred_element_type=F32)).astype(BF16)
+            proj[1, rows, columns] = (part * jnp.dot(left_sin, right, preferred_element_type=F32)).astype(BF16)
+            return carry
+
+        lax.fori_loop(0, width // 256, tile, 0)
+
+    build(1 - y_lo)
+    for copy in loads[:2]:
+        copy.wait()
     pl.semaphore_wait(barrier, nz + nband - 1)
 
     started = []
@@ -216,51 +292,19 @@
     mate_block = band_id(1 - y_hi, x, core)
     x_others = [(x + dx) % nx for dx in range(1, nx)]
     sent = forward(
-        occ_ref,
+        occ_all.at[b],
         b,
         0,
         [mate_block] + [band_id(y_hi, xx, core) for xx in x_others] + [band_id(y_hi, x, 1 - core)],
     )
-    occ_all[b] = occ_ref[...]
-
-    coef[...] = jnp.zeros_like(coef)
-    occ_coef[...] = jnp.zeros_like(occ_coef)
-
-    def project_occ(index, carry):
-        columns = pl.ds(pl.multiple_of(index * 256, 256), 256)
-        occ_coef[...] += dot_t(proj[0, :, columns], occ_a[:, columns]) + dot_t(
-            proj[1, :, columns], occ_b[:, columns]
-        )
-        return carry
-
-    lax.fori_loop(0, width // 256, project_occ, 0)
-    npw = 2 * nz
-    for owner in range(npw):
-        rows = occ_coef[24 * owner : 24 * owner + 24, :] * strength_ref[24 * owner : 24 * owner + 24, :]
-        occ_tile[owner] = (
-            rows[0:8] + pltpu.roll(rows[8:16], 32, 1) + pltpu.roll(rows[16:24], 64, 1)
-        )
-    tile_copy = put(
-        occ_tile.at[pl.ds((1 - y_lo) * nz, nz)], oyr, oy_send.at[0], oy_recv.at[0], y_mate, b
-    )
-    tile_copy.start()
-    block_arrived(mate_block)
-    sent = forward(
-        occ_all.at[mate_block],
-        mate_block,
-        sent,
-        [band_id(y_hi, xx, core) for xx in x_others] + [band_id(y_hi, x, 1 - core)],
-    )
-
-    def project(index, carry):
-        columns = pl.ds(pl.multiple_of(index * 256, 256), 256)
-        real, imag = proj[0, :, columns], proj[1, :, columns]
-        high_r, high_i = high_ref[0, :, columns], high_ref[1, :, columns]
-        coef[0] += dot_t(real, high_r) + dot_t(imag, high_i)
-        coef[1] += dot_t(real, high_i) - dot_t(imag, high_r)
-        return carry
-
-    lax.fori_loop(0, width // 256, project, 0)
+
+    def project(half):
+        rows = pl.ds(pl.multiple_of(half * hrow, hrow), hrow)
+        real, imag = proj[0, rows, :], proj[1, rows, :]
+        coef[0, rows, :] = dot_t(real, high_ref[0]) + dot_t(imag, high_ref[1])
+        coef[1, rows, :] = dot_t(real, high_ref[1]) - dot_t(imag, high_ref[0])
+
+    project(1 - y_lo)
 
     def chunk1(owner):
         return coef[:, pl.ds(pl.multiple_of(owner * 24, 8), 24), :].reshape(48, 256)
@@ -297,39 +341,49 @@
 
         for slot, (offset, target) in enumerate(MOVES):
             push(slot, local(offset), target)
+        fill(0)
         relayed = [local(offset) for offset in RELAYS]
         for place, offset in enumerate(DIRECT):
             push(len(MOVES) + place, local(offset), offset)
-        fill(0)
+        fill(1)
         for place, offset in enumerate(RELAYS):
             value = relayed[place]
             for slot, (_, target) in enumerate(MOVES):
                 if target * offset > 0:
                     value = value + arrived(slot)
             push(len(MOVES) + len(DIRECT) + place, value, offset)
-        fill(1)
+        fill(2)
         value = local(0)
         for place in range(len(DIRECT) + len(RELAYS)):
             value = value + arrived(len(MOVES) + place)
         return value, list(copies.values())
 
     mates1 = mate_sends(chunk1, ys1, yr1, y1_send, y1_recv)
-    tile_copy.wait_recv()
-    spread_copies = []
-    for step in range(1, nz):
-        dest = (z + step) % nz
-        tile_send[step] = occ_tile[pw_id(y_lo, dest)] + oyr[dest]
-        copy = put(
-            tile_send.at[step], tile_recv.at[step], ts_send.at[step], ts_recv.at[step], z_at(step), b
+    build(y_lo)
+    project(y_lo)
+    block_arrived(mate_block)
+    sent = forward(
+        occ_all.at[mate_block],
+        mate_block,
+        sent,
+        [band_id(y_hi, xx, core) for xx in x_others] + [band_id(y_hi, x, 1 - core)],
+    )
+    occ_a[...] = jnp.zeros_like(occ_a)
+    occ_b[...] = jnp.zeros_like(occ_b)
+    occ_a[0:nown, :] = occ_all[b, 0]
+    occ_a[nown : 2 * nown, :] = occ_all[b, 1]
+    occ_b[0:nown, :] = occ_all[b, 1]
+    occ_b[nown : 2 * nown, :] = -occ_all[b, 0]
+    occ_coef[...] = dot_t(proj[0], occ_a[...]) + dot_t(proj[1], occ_b[...])
+    for owner in range(2 * nz):
+        rows = occ_coef[24 * owner : 24 * owner + 24, :] * strength_ref[24 * owner : 24 * owner + 24, :]
+        occ_tile[owner] = (
+            rows[0:8] + pltpu.roll(rows[8:16], 32, 1) + pltpu.roll(rows[16:24], 64, 1)
         )
-        copy.start()
-        spread_copies.append(copy)
-    for yy in (y_hi, 1 - y_hi):
-        for xx in x_others:
-            block = band_id(yy, xx, core)
-            block_arrived(block)
-            sent = forward(occ_all.at[block], block, sent, [band_id(y_hi, x, 1 - core)])
-    total[...] = jnp.zeros_like(total)
+    tile_copy = put(
+        occ_tile.at[pl.ds((1 - y_lo) * nz, nz)], oyr, oy_send.at[0], oy_recv.at[0], y_mate, b
+    )
+    tile_copy.start()
 
     nocc = total.shape[2]
 
@@ -342,13 +396,49 @@
                 scaled[part, axis * nocc : (axis + 1) * nocc, :] = (values * vector).astype(BF16)
         real, imag = scaled[0], scaled[1]
         high_r, high_i = high_ref[0, :, columns], high_ref[1, :, columns]
-        total[0] += (dot_t(real, high_r) + dot_t(imag, high_i)).reshape(3, nocc, 256)
-        total[1] += (dot_t(real, high_i) - dot_t(imag, high_r)).reshape(3, nocc, 256)
+        parts = (
+            dot_t(real, high_r) + dot_t(imag, high_i),
+            dot_t(real, high_i) - dot_t(imag, high_r),
+        )
+        for part in range(2):
+            value = parts[part].reshape(3, nocc, 256)
+            if index == 0:
+                total[part] = value
+            else:
+                total[part] += value
 
     tile_copies = []
+    spread_copies = []
 
     def fill1(point):
+        nonlocal sent
         if point == 0:
+            tile_copy.wait_recv()
+            for step in range(1, nz):
+                dest = (z + step) % nz
+                tile_send[step] = occ_tile[pw_id(y_lo, dest)] + oyr[dest]
+                copy = put(
+                    tile_send.at[step],
+                    tile_recv.at[step],
+                    ts_send.at[step],
+                    ts_recv.at[step],
+                    z_at(step),
+                    b,
+                )
+                copy.start()
+                spread_copies.append(copy)
+            for yy in (y_hi, 1 - y_hi):
+                for xx in x_others:
+                    block = band_id(yy, xx, core)
+                    block_arrived(block)
+                    sent = forward(occ_all.at[block], block, sent, [band_id(y_hi, x, 1 - core)])
+        elif point == 1:
+            for xx in [x] + x_others:
+                for yy in range(2):
+                    block_arrived(band_id(yy, xx, 1 - core))
+            for index in range(3):
+                momentum_piece(index)
+        else:
             tile = occ_tile[p] + oyr[z]
             for copy, step in zip(spread_copies, range(1, nz)):
                 copy.wait_recv()
@@ -361,13 +451,7 @@
                 copy.start()
                 tile_copies.append(copy)
             tiles[b] = tile
-            for xx in [x] + x_others:
-                for yy in range(2):
-                    block_arrived(band_id(yy, xx, 1 - core))
-            momentum_piece(0)
-            momentum_piece(1)
-        else:
-            for index in range(2, width // 256):
+            for index in range(3, width // 256):
                 momentum_piece(index)
 
     high_sum, moves1 = reduce_z(chunk1, mates1, yr1, zs1, zr1, z1_send, z1_recv, fill1)
@@ -414,11 +498,19 @@
             left_hi = left.astype(BF16)
             left_lo = (left - left_hi.astype(F32)).astype(BF16)
             lhs = jnp.concatenate([left_hi, left_hi, left_lo], axis=0)
-            total[part, axis] += lax.dot_general(
-                lhs, rhs, (((0,), (0,)), ((), ())), preferred_element_type=F32
-            )
-
+            lefts[3 * part + axis] = lhs
+
+    def nonlocal_part(half):
+        rows = pl.ds(pl.multiple_of(half * (nocc // 2), 128), nocc // 2)
+        for part in range(2):
+            for axis in range(3):
+                total[part, axis, rows, :] += lax.dot_general(
+                    lefts[3 * part + axis, :, rows], rhs, (((0,), (0,)), ((), ())), preferred_element_type=F32
+                )
+
+    nonlocal_part(1 - y_lo)
     mates2 = mate_sends(chunk2, ys2, yr2, y2_send, y2_recv)
+    nonlocal_part(y_lo)
     result, moves2 = reduce_z(
         chunk2, mates2, yr2, zs2, zr2, z2_send, z2_recv, lambda point: None
     )
@@ -436,24 +528,38 @@
 def on_device(
     nz, nx, psi_occ, psi_high, miller, recip, kfrac, positions, atom_type, proj_atom, widths, dion
 ):
-    nproj = proj_atom.shape[0]
+    nproj, natom, ntype = proj_atom.shape[0], positions.shape[0], widths.shape[0]
     nown, nhigh, width = psi_occ.shape[1], psi_high.shape[1], psi_high.shape[2]
     npw, nband = 2 * nz, 4 * nx
     nocc = nown * nband
-    table = projector_table(positions, atom_type, proj_atom, widths, dion)
-    strength = jnp.broadcast_to(jnp.repeat(table[:, 4:5], 4, axis=0), (4 * nproj, 128))
-    vmem, smem = pltpu.VMEM, pltpu.SMEM
+    vmem = pltpu.VMEM
     dma = pltpu.SemaphoreType.DMA
     out = pl.pallas_call(
         functools.partial(kernel, nz, nx),
         out_shape=jax.ShapeDtypeStruct((3, 2, nocc // npw, nhigh), F32),
-        in_specs=[pl.BlockSpec(memory_space=vmem)] * 5 + [pl.BlockSpec(memory_space=smem)] * 2,
+        in_specs=[pl.BlockSpec(memory_space=pltpu.HBM)] * 10,
         out_specs=pl.BlockSpec(memory_space=vmem),
         scratch_shapes=[
+            vmem((2, nhigh, width), BF16),
+            vmem((3, width), jnp.int32),
+            vmem((3, 3), F32),
+            vmem((1, 3), F32),
+            vmem((3, natom), F32),
+            vmem((1, natom), jnp.int32),
+            vmem((1, nproj), jnp.int32),
+            vmem((1, ntype), F32),
+            vmem((1, ntype), F32),
+            dma((10,)),
             vmem((nband, 2, nown, width), BF16),
             vmem((4, 8, width), F32),
-            vmem((2, LANES // 128, 32, 128), F32),
+            vmem((4 * natom, width), BF16),
+            vmem((ntype, 16, width), F32),
+            vmem((4 * nproj, 4 * natom), BF16),
+            vmem((4 * nproj, 4 * natom), BF16),
+            vmem((4 * nproj, 8), F32),
+            vmem((4 * nproj, 128), F32),
             vmem((2, 4 * nproj, width), BF16),
+            vmem((6, 144, nocc), BF16),
             vmem((128, width), BF16),
             vmem((128, width), BF16),
             vmem((2, 4 * nproj, nhigh), F32),
@@ -494,7 +600,18 @@
         compiler_params=pltpu.CompilerParams(
             collective_id=0, has_side_effects=True, vmem_limit_bytes=52 * 1024 * 1024
         ),
-    )(psi_occ, psi_high, miller, table, strength, recip, kfrac)
+    )(
+        psi_occ,
+        psi_high,
+        miller,
+        recip,
+        kfrac[None],
+        positions.T,
+        atom_type[None],
+        proj_atom[None],
+        widths[None],
+        dion[None],
+    )
     return out
 
 

time: 71.4 us -> 71.7 us (level)
  the two profiles are of different devices: /device:TPU:2 before, /device:TPU:1 now
where the time goes in v3:
time: 71.7 us; the launch traced here: 70.3 us
  Pallas kernels  62 us (86%)
  local copies, waits for them, and re-layouts  8.32 us (12%)
    pallas_call x1, Pallas kernels, on_device(): pl.pallas_call(functools.partial(kernel, nz, nx), out_shape=jax.ShapeDtyp...  62 us
    unnamed x21, local copies, waits for them, and re-layouts  8.32 us

profile of v3, /device:TPU:1, one launch (start us, length us, event | category | flops | bytes accessed | tf_op | source)
XLA Modules:
  0.0 70.3 jit_solution(9284850243972517569)
XLA Ops:
  0.0 0.0 copy-start
  0.0 1.4 %copy-done = bf16[2,256,1536]{2,1,0:T(8,128)(2,1)S(1)} copy-done((bf16[2,256,1536]{2,1,0:T(8,128)(2,1)S(1)}, bf16[2,256,1536]{2,1,0:T(8,128)(2,1)}, u32[]{:S(2)}) %copy-start) | copy-done | bytes 1572888
  1.4 0.0 copy-start.1
  1.4 0.9 %copy-done.1 = bf16[2,16,1536]{2,1,0:T(8,128)(2,1)S(1)} copy-done((bf16[2,16,1536]{2,1,0:T(8,128)(2,1)S(1)}, bf16[2,16,1536]{2,1,0:T(8,128)(2,1)}, u32[]{:S(2)}) %copy-start.1) | copy-done | bytes 98328
  2.3 0.0 copy-start.2
  2.3 0.7 %copy-done.2 = s32[3,1536]{1,0:T(4,128)S(1)} copy-done((s32[3,1536]{1,0:T(4,128)S(1)}, s32[3,1536]{1,0:T(4,128)}, u32[]{:S(2)}) %copy-start.2) | copy-done | bytes 18456
  3.0 0.0 copy-start.3
  3.0 0.7 copy-done.3
  3.7 0.0 copy-start.4
  3.7 0.7 copy-done.4
  4.4 0.0 copy-start.5
  4.4 0.7 copy-done.5
  5.1 0.0 copy-start.6
  5.1 0.7 copy-done.6
  5.7 0.0 copy-start.7
  5.7 0.7 copy-done.7
  6.4 0.0 copy-start.8
  6.4 0.7 copy-done.8
  7.1 0.0 copy-start.9
  7.1 0.7 copy-done.9
  7.7 62.0 %shard_map.100 = f32[3,2,8,256]{3,2,1,0:T(8,128)S(1)} custom-call(bf16[2,16,1536]{2,1,0:T(8,128)(2,1)S(1)} %copy-done.1, bf16[2,256,1536]{2,1,0:T(8,128)(2,1)S(1)} %copy-done, s32[3,1536]{1,0:T(4,128)S(1)} %copy-done.2, f32[3,3]{1,0:T(4,128)S(1)} %copy-done.3, f32[1,3]{1,0:T(1,128)S(1)} %bitcast.8, f32[3,48]{1,0:T(4,128)S(1)} %bitcast.6, ...), custom_call_target="tpu_custom_call" | custom-call | tf_op jit(solution)/shard_map/pallas_call | solution.py:537
  69.7 0.6 copy.12
Async XLA Ops:
  0.0 1.4 %copy-start = (bf16[2,256,1536]{2,1,0:T(8,128)(2,1)S(1)}, bf16[2,256,1536]{2,1,0:T(8,128)(2,1)}, u32[]{:S(2)}) copy-start(bf16[2,256,1536]{2,1,0:T(8,128)(2,1)} %high_hbm.1) | copy-start | bytes 4718596
  1.4 0.9 %copy-start.1 = (bf16[2,16,1536]{2,1,0:T(8,128)(2,1)S(1)}, bf16[2,16,1536]{2,1,0:T(8,128)(2,1)}, u32[]{:S(2)}) copy-start(bf16[2,16,1536]{2,1,0:T(8,128)(2,1)} %occ_hbm.1) | copy-start | bytes 294916
  2.3 0.7 %copy-start.2 = (s32[3,1536]{1,0:T(4,128)S(1)}, s32[3,1536]{1,0:T(4,128)}, u32[]{:S(2)}) copy-start(s32[3,1536]{1,0:T(4,128)} %miller_hbm.1) | copy-start | bytes 55300
  3.0 0.7 copy-start.3
  3.7 0.7 copy-start.4
  4.4 0.7 copy-start.5
  5.1 0.7 copy-start.6
  5.7 0.7 copy-start.7
  6.4 0.7 copy-start.8
  7.1 0.7 copy-start.9

commit v4 on v3

--- a/solution.py
+++ b/solution.py
@@ -87,7 +87,6 @@
     total,
     ys1,
     yr1,
-    oyr,
     zs1,
     zr1,
     ys2,
@@ -102,8 +101,6 @@
     g_recv,
     y1_send,
     y1_recv,
-    oy_send,
-    oy_recv,
     ts_send,
     ts_recv,
     z1_send,
@@ -122,6 +119,8 @@
     y_hi, x, core = b // (2 * nx), (b // 2) % nx, b % 2
     width, nown = high_hbm.shape[2], occ_hbm.shape[1]
 
+    odd = z % 2
+
     def band_id(yy, xx, cc):
         return yy * (2 * nx) + xx * 2 + cc
 
@@ -162,7 +161,10 @@
     for copy in loads[2:] + loads[:2]:
         copy.start()
     barrier = pltpu.get_barrier_semaphore()
-    pl.semaphore_signal(barrier, inc=1, device_id={"pw": y_mate, "band": b}, device_id_type=MESH)
+    for step in range(nband):
+        pl.semaphore_signal(
+            barrier, inc=1, device_id={"pw": y_mate, "band": (b + step) % nband}, device_id_type=MESH
+        )
     for step in range(1, nz):
         pl.semaphore_signal(
             barrier, inc=1, device_id={"pw": z_at(step), "band": b}, device_id_type=MESH
@@ -274,7 +276,7 @@
     build(1 - y_lo)
     for copy in loads[:2]:
         copy.wait()
-    pl.semaphore_wait(barrier, nz + nband - 1)
+    pl.semaphore_wait(barrier, nz - 1 + 2 * nband - 1)
 
     started = []
 
@@ -340,16 +342,18 @@
             return zr[slot].astype(F32)
 
         for slot, (offset, target) in enumerate(MOVES):
-            push(slot, local(offset), target)
+            push(slot, local(offset), target if slot else 4 - 8 * odd)
         fill(0)
         relayed = [local(offset) for offset in RELAYS]
         for place, offset in enumerate(DIRECT):
             push(len(MOVES) + place, local(offset), offset)
         fill(1)
+        farthest = arrived(0)
         for place, offset in enumerate(RELAYS):
-            value = relayed[place]
+            share = odd if place else 1 - odd
+            value = relayed[place] + farthest * share.astype(F32)
             for slot, (_, target) in enumerate(MOVES):
-                if target * offset > 0:
+                if slot and target * offset > 0:
                     value = value + arrived(slot)
             push(len(MOVES) + len(DIRECT) + place, value, offset)
         fill(2)
@@ -380,10 +384,17 @@
         occ_tile[owner] = (
             rows[0:8] + pltpu.roll(rows[8:16], 32, 1) + pltpu.roll(rows[16:24], 64, 1)
         )
-    tile_copy = put(
-        occ_tile.at[pl.ds((1 - y_lo) * nz, nz)], oyr, oy_send.at[0], oy_recv.at[0], y_mate, b
-    )
-    tile_copy.start()
+    def both_halves(dest):
+        return jnp.concatenate([occ_tile[dest], occ_tile[nz + dest]], axis=0)
+
+    spread_copies = []
+    for step in range(1, nz):
+        tile_send[step] = both_halves((z + step) % nz).astype(BF16)
+        copy = put(
+            tile_send.at[step], tile_recv.at[step], ts_send.at[step], ts_recv.at[step], z_at(step), b
+        )
+        copy.start()
+        spread_copies.append(copy)
 
     nocc = total.shape[2]
 
@@ -408,25 +419,10 @@
                 total[part] += value
 
     tile_copies = []
-    spread_copies = []
 
     def fill1(point):
         nonlocal sent
         if point == 0:
-            tile_copy.wait_recv()
-            for step in range(1, nz):
-                dest = (z + step) % nz
-                tile_send[step] = occ_tile[pw_id(y_lo, dest)] + oyr[dest]
-                copy = put(
-                    tile_send.at[step],
-                    tile_recv.at[step],
-                    ts_send.at[step],
-                    ts_recv.at[step],
-                    z_at(step),
-                    b,
-                )
-                copy.start()
-                spread_copies.append(copy)
             for yy in (y_hi, 1 - y_hi):
                 for xx in x_others:
                     block = band_id(yy, xx, core)
@@ -439,18 +435,36 @@
             for index in range(3):
                 momentum_piece(index)
         else:
-            tile = occ_tile[p] + oyr[z]
+            tile = both_halves(z)
             for copy, step in zip(spread_copies, range(1, nz)):
                 copy.wait_recv()
-                tile = tile + tile_recv[step]
-            tile_own[...] = tile
-            for step in range(1, nband):
+                tile = tile + tile_recv[step].astype(F32)
+            tile_own[0] = tile[0:8]
+            tile_own[1] = tile[8:16]
+            for step in range(nband):
+                band = (b + step) % nband
                 copy = put(
-                    tile_own, tiles.at[b], t_send.at[step - 1], t_recv.at[b], p, (b + step) % nband
+                    tile_own.at[1 - y_lo],
+                    tiles.at[y_lo, b],
+                    t_send.at[1, step],
+                    t_recv.at[y_lo, b],
+                    y_mate,
+                    band,
                 )
                 copy.start()
                 tile_copies.append(copy)
-            tiles[b] = tile
+                if step:
+                    copy = put(
+                        tile_own.at[y_lo],
+                        tiles.at[y_lo, b],
+                        t_send.at[0, step],
+                        t_recv.at[y_lo, b],
+                        p,
+                        band,
+                    )
+                    copy.start()
+                    tile_copies.append(copy)
+            tiles[y_lo, b] = tile_own[y_lo]
             for index in range(3, width // 256):
                 momentum_piece(index)
 
@@ -459,9 +473,12 @@
     high_hi = high_sum.astype(BF16)
     high_lo = (high_sum - high_hi.astype(F32)).astype(BF16)
     rhs = jnp.concatenate([high_hi, high_lo, high_hi], axis=0)
-    for step in range(1, nband):
+    for step in range(nband):
         block = (b + step) % nband
-        put(tile_own, tiles.at[block], t_send.at[0], t_recv.at[block], p, b).wait_recv()
+        for side in ([y_lo, 1 - y_lo] if step else [1 - y_lo]):
+            put(
+                tile_own.at[0], tiles.at[side, block], t_send.at[0, 0], t_recv.at[side, block], p, b
+            ).wait_recv()
 
     lane_block = lax.broadcasted_iota(jnp.int32, (8, 128), 1) // 16
     occ_sums = []
@@ -473,7 +490,7 @@
                 value = jnp.zeros((8, 128), F32)
                 for place in range(8):
                     shift = (16 * place - 32 * group - 16 * part) % 128
-                    tile = tiles[8 * side + place]
+                    tile = tiles[0, 8 * side + place] + tiles[1, 8 * side + place]
                     if shift:
                         tile = pltpu.roll(tile, shift, 1)
                     value = jnp.where(lane_block == place, tile, value)
@@ -520,7 +537,7 @@
             out_ref[axis, part] = result[part, axis]
 
     for copy in (
-        started + [tile_copy] + mates1 + spread_copies + moves1 + tile_copies + mates2 + moves2
+        started + mates1 + spread_copies + moves1 + tile_copies + mates2 + moves2
     ):
         copy.wait_send()
 
@@ -569,23 +586,20 @@
             vmem((2, 3, nocc, nhigh), F32),
             vmem((nz, 48, nhigh), BF16),
             vmem((nz, 48, nhigh), BF16),
-            vmem((nz, 8, 128), F32),
             vmem((nz - 1, 48, nhigh), BF16),
             vmem((nz - 1, 48, nhigh), BF16),
             vmem((nz, 48, nhigh), BF16),
             vmem((nz, 48, nhigh), BF16),
             vmem((nz - 1, 48, nhigh), BF16),
             vmem((nz - 1, 48, nhigh), BF16),
-            vmem((nz, 8, 128), F32),
-            vmem((nz, 8, 128), F32),
-            vmem((8, 128), F32),
-            vmem((nband, 8, 128), F32),
+            vmem((nz, 16, 128), BF16),
+            vmem((nz, 16, 128), BF16),
+            vmem((2, 8, 128), F32),
+            vmem((2, nband, 8, 128), F32),
             dma((nband - 1,)),
             dma((nband,)),
             dma((nz,)),
             dma((nz,)),
-            dma((1,)),
-            dma((1,)),
             dma((nz,)),
             dma((nz,)),
             dma((nz - 1,)),
@@ -594,11 +608,11 @@
             dma((nz,)),
             dma((nz - 1,)),
             dma((nz - 1,)),
-            dma((nband - 1,)),
-            dma((nband,)),
+            dma((2, nband)),
+            dma((2, nband)),
         ],
         compiler_params=pltpu.CompilerParams(
-            collective_id=0, has_side_effects=True, vmem_limit_bytes=52 * 1024 * 1024
+            collective_id=0, has_side_effects=True, vmem_limit_bytes=64 * 1024 * 1024
         ),
     )(
         psi_occ,

time: 71.7 us -> 61.9 us (0.86); the launches traced: 70.3 us -> 61.8 us
  local copies, waits for them, and re-layouts: 8.32 us -> 1.42 us
  Pallas kernels: 62 us -> 60.3 us
    unnamed x21 -> x1, local copies, waits for them, and re-layouts: 8.32 us -> 1.42 us
    pallas_call x1, Pallas kernels: 62 us -> 60.3 us  [on_device(): pl.pallas_call(functools.partial(kernel, nz, nx), out_shape=jax.ShapeDtyp...]
where the time goes in v4:
time: 61.9 us; the launch traced here: 61.8 us
  Pallas kernels  60.3 us (97%)
  local copies, waits for them, and re-layouts  1.42 us (2%)
    pallas_call x1, Pallas kernels, on_device(): pl.pallas_call(functools.partial(kernel, nz, nx), out_shape=jax.ShapeDtyp...  60.3 us
    unnamed x1, local copies, waits for them, and re-layouts  1.42 us

profile of v4, /device:TPU:1, one launch (start us, length us, event | category | flops | bytes accessed | tf_op | source)
XLA Modules:
  0.0 61.8 jit_solution(11675793932282893254)
XLA Ops:
  0.0 60.3 %shard_map.100 = f32[3,2,8,256]{3,2,1,0:T(8,128)} custom-call(bf16[2,16,1536]{2,1,0:T(8,128)(2,1)} %occ_hbm.1, bf16[2,256,1536]{2,1,0:T(8,128)(2,1)} %high_hbm.1, s32[3,1536]{1,0:T(4,128)} %miller_hbm.1, f32[3,3]{1,0:T(4,128)} %recip_hbm.1, f32[1,3]{1,0:T(1,128)} %bitcast.8, f32[3,48]{1,0:T(4,128)} %bitcast.6, s32[1,48]{1,0:T(1,128)} %bitcast.9, ...), custom_call_target="tpu_custom_call" | custom-call | tf_op jit(solution)/shard_map/pallas_call | solution.py:554
  60.3 1.4 %copy.12 = f32[3,2,8,256]{3,2,1,0:T(8,128)} copy(f32[3,2,8,256]{3,2,1,0:T(8,128)} %shard_map.100) | data formatting | bytes 98304

commit v5 on v4

--- a/solution.py
+++ b/solution.py
@@ -434,7 +434,6 @@
                     block_arrived(band_id(yy, xx, 1 - core))
             for index in range(3):
                 momentum_piece(index)
-        else:
             tile = both_halves(z)
             for copy, step in zip(spread_copies, range(1, nz)):
                 copy.wait_recv()
@@ -465,6 +464,7 @@
                     copy.start()
                     tile_copies.append(copy)
             tiles[y_lo, b] = tile_own[y_lo]
+        else:
             for index in range(3, width // 256):
                 momentum_piece(index)
 

time: 61.9 us -> 59.2 us (0.956)
  Pallas kernels: 60.3 us -> 57.5 us
    pallas_call x1, Pallas kernels: 60.3 us -> 57.5 us  [on_device(): pl.pallas_call(functools.partial(kernel, nz, nx), out_shape=jax.ShapeDtyp...]
where the time goes in v5:
time: 59.2 us; the launch traced here: 59 us
  Pallas kernels  57.5 us (97%)
  local copies, waits for them, and re-layouts  1.42 us (2%)
    pallas_call x1, Pallas kernels, on_device(): pl.pallas_call(functools.partial(kernel, nz, nx), out_shape=jax.ShapeDtyp...  57.5 us
    unnamed x1, local copies, waits for them, and re-layouts  1.42 us

profile of v5, /device:TPU:1, one launch (start us, length us, event | category | flops | bytes accessed | tf_op | source)
XLA Modules:
  0.0 59.0 jit_solution(1249518714698673304)
XLA Ops:
  0.0 57.5 %shard_map.100 = f32[3,2,8,256]{3,2,1,0:T(8,128)} custom-call(bf16[2,16,1536]{2,1,0:T(8,128)(2,1)} %occ_hbm.1, bf16[2,256,1536]{2,1,0:T(8,128)(2,1)} %high_hbm.1, s32[3,1536]{1,0:T(4,128)} %miller_hbm.1, f32[3,3]{1,0:T(4,128)} %recip_hbm.1, f32[1,3]{1,0:T(1,128)} %bitcast.8, f32[3,48]{1,0:T(4,128)} %bitcast.6, s32[1,48]{1,0:T(1,128)} %bitcast.9, ...), custom_call_target="tpu_custom_call" | custom-call | tf_op jit(solution)/shard_map/pallas_call | solution.py:554
  57.6 1.4 %copy.12 = f32[3,2,8,256]{3,2,1,0:T(8,128)} copy(f32[3,2,8,256]{3,2,1,0:T(8,128)} %shard_map.100) | data formatting | bytes 98304
